TPU v7x, 32 devices: a whole 2x2x4 slice. The times are simulated.
32 devices in a mesh: segment: 2 (over x), seq: 4 (over y, core), head: 4 (over z).
Axes of the slice: x: 2, y: 2, z: 4, core: 2. Of those that a mesh axis runs over, the one named last changes fastest.
Arguments:
- stream: bfloat16 [2, 512, 4096], P(None, 'seq', 'head'), may hold values from -6 to 6
- in_gain: float32 [2, 4096], P('segment'), may hold values from 0.25 to 1.75
- w_qkv: bfloat16 [2, 4096, 4, 3, 512], P('segment', None, 'head'), may hold values from -0.09375 to 0.09375
- qk_gain: float32 [2, 4, 2, 512], P('segment', 'head'), may hold values from 0.25 to 1.75
- w_one: bfloat16 [2, 4, 512, 768], P('segment', 'head'), may hold values from -0.25 to 0.25
- w_three: bfloat16 [2, 4, 512, 768], P('segment', 'head'), may hold values from -0.25 to 0.25
- w_two: bfloat16 [2, 4, 768, 512], P('segment', 'head'), may hold values from -0.21875 to 0.21875
- token_rate: float32 [2, 2, 512], P('segment', None, 'seq'), may hold values from 0.05 to 1
- out_gain: float32 [2, 4, 512], P('segment', 'head'), may hold values from 0.25 to 1.75
- w_out: bfloat16 [2, 4, 512, 4096], P('segment', 'head'), may hold values from -0.125 to 0.125
Outputs:
- sections_out: bfloat16 [2, 2, 512, 4096], P('segment', None, 'seq', 'head')
All inputs are finite; a program needn't handle non-finite values.
Results may differ from a plain program's by a relative error of at most 0.038.
Values may be sent and summed in bfloat16 or wider, within the bound.
A program may use at most 128 MiB of HBM per device.

v0:
```python
import functools

import jax
import jax.numpy as jnp
from jax import lax
from jax.experimental import pallas as pl
from jax.experimental.pallas import tpu as pltpu
from jax.sharding import PartitionSpec as P

NS_STEPS = 2


ns_first = 3.4445
ns_second = -4.775
ns_third = 2.0315
update_step = 1.0
norm_eps = 1e-06
grad_eps = 1e-07


def rms_scale(values):
    return values * lax.rsqrt(jnp.mean(values * values, axis=-1, keepdims=True) + norm_eps)


def dot(left, right):
    return jnp.dot(left, right, preferred_element_type=jnp.float32)


def contract(left, right, dims):
    return lax.dot_general(
        left, right, ((dims[:1], dims[1:]), ((), ())), preferred_element_type=jnp.float32
    )


def fast_kernel(
    active_ref,
    both_ref,
    query_ref,
    gate_ref,
    up_ref,
    down_ref,
    wide_norms_ref,
    down_norm_ref,
    out_gain_ref,
    out_weights_hbm,
    terms_ref,
    new_gate_ref,
    new_up_ref,
    new_down_ref,
    rights,
    work,
    out_weights,
    out_sem,
):
    fetch = pltpu.make_async_copy(out_weights_hbm, out_weights, out_sem)
    fetch.start()
    tokens = both_ref.shape[1]
    rows = query_ref.shape[0]
    chunk = 2 * rows if tokens % (2 * rows) == 0 else rows
    work[0] = gate_ref[...].astype(jnp.bfloat16)
    work[1] = up_ref[...].astype(jnp.bfloat16)
    work[2] = down_ref[...].astype(jnp.bfloat16)

    def gradients(index, carry):
        here = pl.ds(pl.multiple_of(index * chunk, chunk), chunk)
        keys = both_ref[0, here, :]
        grads = both_ref[1, here, :]
        pre_gate = dot(keys, work[0])
        pre_up = dot(keys, work[1])
        backward = dot(grads, work[2])
        sigmoid_gate = jax.nn.sigmoid(pre_gate)
        gated = pre_gate * sigmoid_gate
        rights[0, here, :] = (
            backward * pre_up * sigmoid_gate * (1.0 + pre_gate * (1.0 - sigmoid_gate))
        ).astype(jnp.bfloat16)
        rights[1, here, :] = (backward * gated).astype(jnp.bfloat16)
        rights[2, here, :] = (gated * pre_up).astype(jnp.bfloat16)
        return carry

    lax.fori_loop(0, tokens // chunk, gradients, 0)

    def orthogonalize(index, carry):
        gradient = contract(both_ref[index // 2], rights[index], (0, 0))
        scale = 1.0 / (jnp.sqrt(jnp.sum(gradient * gradient, keepdims=True)) + grad_eps)
        work[index] = (gradient * scale).astype(jnp.bfloat16)

        def sweep(step, inner):
            current = work[index]
            gram_matrix = contract(current, current, (1, 1)).astype(jnp.bfloat16)
            square = dot(gram_matrix, gram_matrix)
            mixing = (ns_second * gram_matrix.astype(jnp.float32) + ns_third * square).astype(
                jnp.bfloat16
            )
            work[index] = (ns_first * current.astype(jnp.float32) + dot(mixing, current)).astype(
                jnp.bfloat16
            )
            return inner

        return lax.fori_loop(0, NS_STEPS, sweep, carry)

    lax.fori_loop(0, 3, orthogonalize, 0)

    active = active_ref[0] > 0
    for index, old_ref, new_ref, axis, target in (
        (0, gate_ref, new_gate_ref, 0, wide_norms_ref[0]),
        (1, up_ref, new_up_ref, 0, wide_norms_ref[1]),
        (2, down_ref, new_down_ref, 1, down_norm_ref[...]),
    ):
        moved = old_ref[...] - update_step * work[index].astype(jnp.float32)
        length = jnp.sqrt(jnp.sum(moved * moved, axis=axis, keepdims=True)) + norm_eps
        fresh = moved * (target / length)
        work[index] = fresh.astype(jnp.bfloat16)
        new_ref[...] = jnp.where(active, fresh, old_ref[...])

    gate_out = dot(query_ref[...], work[0])
    up_out = dot(query_ref[...], work[1])
    inner = (gate_out * jax.nn.sigmoid(gate_out) * up_out).astype(jnp.bfloat16)
    output = contract(inner, work[2], (1, 1))
    normed_out = (rms_scale(output) * out_gain_ref[...]).astype(jnp.bfloat16)
    fetch.wait()
    width = terms_ref.shape[2]

    def project(index, carry):
        columns = pl.ds(pl.multiple_of(index * width, width), width)
        terms_ref[index] = dot(normed_out, out_weights[:, columns]).astype(jnp.bfloat16)
        return carry

    lax.fori_loop(0, terms_ref.shape[0], project, 0)


def fast_step(active, both, queries, fasts, norms, out_gain_row, out_weights, heads):
    rows = queries.shape[0]
    inner, wide = fasts[0].shape
    width = out_weights.shape[1] // heads
    vmem = pl.BlockSpec(memory_space=pltpu.VMEM)
    state = jax.ShapeDtypeStruct((inner, wide), jnp.float32)
    held = 4 * both.size + 6 * both.shape[1] * wide + 30 * inner * wide + 2 * out_weights.size
    return pl.pallas_call(
        fast_kernel,
        name="fast_step",
        out_shape=(jax.ShapeDtypeStruct((heads, rows, width), jnp.bfloat16), state, state, state),
        in_specs=[pl.BlockSpec(memory_space=pltpu.SMEM)]
        + [vmem] * 8
        + [pl.BlockSpec(memory_space=pl.ANY)],
        out_specs=(vmem,) * 4,
        scratch_shapes=[
            pltpu.VMEM((3, both.shape[1], wide), jnp.bfloat16),
            pltpu.VMEM((3, inner, wide), jnp.bfloat16),
            pltpu.VMEM(out_weights.shape, jnp.bfloat16),
            pltpu.SemaphoreType.DMA,
        ],
        compiler_params=pltpu.CompilerParams(vmem_limit_bytes=held + 14 * 1024 * 1024),
        cost_estimate=pl.CostEstimate(
            flops=10**10, bytes_accessed=2 * 10**7, transcendentals=0
        ),
    )(active, both, queries, *fasts, *norms, out_gain_row, out_weights)


def signal(semaphore, target):
    pl.semaphore_signal(
        semaphore, inc=1, device_id=target, device_id_type=pl.DeviceIdType.MESH
    )


def remote(source, target, send_sem, recv_sem, device):
    return pltpu.make_async_remote_copy(
        src_ref=source,
        dst_ref=target,
        send_sem=send_sem,
        recv_sem=recv_sem,
        device_id=device,
        device_id_type=pl.DeviceIdType.MESH,
    )


def gather_tokens_kernel(devices, own_ref, all_ref, send_sems, recv_sems, pair_sends, pair_recvs, own_sem):
    me = lax.axis_index("seq")
    chips = devices // 2
    chip, core = me // 2, lax.rem(me, 2)
    partner = {"seq": 2 * chip + 1 - core}
    parts, rows = own_ref.shape[0], own_ref.shape[1]
    barrier = pltpu.get_barrier_semaphore()
    signal(barrier, partner)
    for step in range(1, chips):
        signal(barrier, {"seq": 2 * lax.rem(chip + step, chips) + core})
    pl.semaphore_wait(barrier, chips)

    def place(part, origin):
        return all_ref.at[part, pl.ds(pl.multiple_of(origin * rows, rows), rows), :]

    far, near = {}, {}
    for part in range(parts):
        for step in range(1, chips):
            far[part, step] = remote(
                own_ref.at[part],
                place(part, me),
                send_sems.at[part, step],
                recv_sems.at[part, step],
                {"seq": 2 * lax.rem(chip + step, chips) + core},
            )
            far[part, step].start()
        near[part, 0] = remote(
            own_ref.at[part], place(part, me), pair_sends.at[part, 0], pair_recvs.at[part, 0], partner
        )
        near[part, 0].start()
    copies = []
    for part in range(parts):
        copies.append(pltpu.make_async_copy(own_ref.at[part], place(part, me), own_sem.at[part]))
        copies[-1].start()
    for part in range(parts):
        for step in range(1, chips):
            far[part, step].wait_recv()
            origin = 2 * lax.rem(chip + chips - step, chips) + core
            near[part, step] = remote(
                place(part, origin),
                place(part, origin),
                pair_sends.at[part, step],
                pair_recvs.at[part, step],
                partner,
            )
            near[part, step].start()
    for copy in copies:
        copy.wait()
    for copy in far.values():
        copy.wait_send()
    for copy in near.values():
        copy.wait_send()
        copy.wait_recv()


def gather_tokens(own):
    devices = lax.axis_size("seq")
    parts, rows, width = own.shape
    vmem = pl.BlockSpec(memory_space=pltpu.VMEM)
    return pl.pallas_call(
        functools.partial(gather_tokens_kernel, devices),
        name="gather_tokens",
        out_shape=jax.ShapeDtypeStruct((parts, devices * rows, width), own.dtype),
        in_specs=[vmem],
        out_specs=vmem,
        scratch_shapes=[pltpu.SemaphoreType.DMA((parts, devices // 2))] * 4
        + [pltpu.SemaphoreType.DMA((parts,))],
        compiler_params=pltpu.CompilerParams(
            collective_id=0, has_side_effects=True, vmem_limit_bytes=16 * 1024 * 1024
        ),
    )(own)


def exchange_kernel(heads, segments, chunks, onward, *refs):
    if onward:
        terms_ref, residual_ref, stream_ref, result_ref, whole_ref = refs[:5]
        slots, total, sum_sends, sum_recvs, copy_sends, copy_recvs, hop_sends, hop_recvs, own_sem = refs[5:]
    else:
        terms_ref, residual_ref, result_ref, slots, total, sum_sends, sum_recvs = refs
    me = lax.axis_index("head")
    segment = lax.axis_index("segment")
    rows, width = residual_ref.shape
    piece = rows // chunks
    has_left, has_right = me >= 1, me + 1 < heads
    barrier = pltpu.get_barrier_semaphore()
    awaited = has_left.astype(jnp.int32) + has_right.astype(jnp.int32)

    @pl.when(has_left)
    def _():
        signal(barrier, {"head": me - 1})

    @pl.when(has_right)
    def _():
        signal(barrier, {"head": me + 1})

    if onward:
        awaited = awaited + (segment + 1 < segments).astype(jnp.int32)

        @pl.when(segment >= 1)
        def _():
            signal(barrier, {"segment": segment - 1})

    pl.semaphore_wait(barrier, awaited)

    def rows_of(chunk):
        return pl.ds(chunk * piece, piece)

    def within(position):
        return (position >= 0) & (position < heads)

    sides = ((0, 1), (1, -1))

    def sum_copy(side, sign, distance, chunk, first):
        source = (
            terms_ref.at[me + sign * distance, rows_of(chunk), :]
            if first
            else slots.at[side, distance, rows_of(chunk), :]
        )
        return remote(
            source,
            slots.at[side, distance - 1, rows_of(chunk), :],
            sum_sends.at[side, distance, chunk],
            sum_recvs.at[side, distance - 1, chunk],
            {"head": me + sign},
        )

    def sum_arrival(side, sign, distance, chunk):
        return remote(
            slots.at[side, distance, rows_of(chunk), :],
            slots.at[side, distance, rows_of(chunk), :],
            sum_sends.at[side, distance, chunk],
            sum_recvs.at[side, distance, chunk],
            {"head": me - sign},
        )

    def send_sums(distance, chunk):
        for side, sign in sides:

            @pl.when(within(me + sign * distance) & jnp.logical_not(within(me - sign)))
            def _():
                sum_copy(side, sign, distance, chunk, True).start()

            if distance < heads - 1:

                @pl.when(within(me + sign * distance) & within(me - sign))
                def _():
                    sum_arrival(side, sign, distance, chunk).wait_recv()
                    here = rows_of(chunk)
                    slots[side, distance, here, :] = (
                        slots[side, distance, here, :].astype(jnp.float32)
                        + terms_ref[me + sign * distance, here, :].astype(jnp.float32)
                    ).astype(jnp.bfloat16)
                    sum_copy(side, sign, distance, chunk, False).start()

    def finish(chunk):
        here = rows_of(chunk)
        total[...] = residual_ref[here, :].astype(jnp.float32) + terms_ref[me, here, :].astype(
            jnp.float32
        )
        for side, sign in sides:

            @pl.when(within(me - sign))
            def _():
                sum_arrival(side, sign, 0, chunk).wait_recv()
                total[...] += slots[side, 0, here, :].astype(jnp.float32)

        result_ref[here, :] = total[...].astype(jnp.bfloat16)
        if onward:

            @pl.when(segment + 1 < segments)
            def _():
                hop(chunk).start()

    def place(origin, chunk):
        return whole_ref.at[
            rows_of(chunk), pl.ds(pl.multiple_of(origin * width, width), width)
        ]

    def hop(chunk):
        return remote(
            result_ref.at[rows_of(chunk), :],
            place(me, chunk),
            hop_sends.at[chunk],
            hop_recvs.at[chunk],
            {"segment": segment + 1},
        )

    def hop_arrival(chunk):
        return remote(
            place(me, chunk),
            place(me, chunk),
            hop_sends.at[chunk],
            hop_recvs.at[chunk],
            {"segment": segment - 1},
        )

    def block_copy(side, sign, step, chunk):
        origin = me - sign * step
        return remote(
            place(origin, chunk),
            place(origin, chunk),
            copy_sends.at[side, step, chunk],
            copy_recvs.at[side, step, chunk],
            {"head": me + sign},
        )

    def block_arrival(side, sign, step, chunk):
        origin = me - sign * (step + 1)
        return remote(
            place(origin, chunk),
            place(origin, chunk),
            copy_sends.at[side, step, chunk],
            copy_recvs.at[side, step, chunk],
            {"head": me - sign},
        )

    def send_blocks(step, chunk):
        if step == 0:

            @pl.when(segment >= 1)
            def _():
                hop_arrival(chunk).wait_recv()

        for side, sign in sides:
            if step > 0:

                @pl.when(within(me - sign * step))
                def _():
                    block_arrival(side, sign, step - 1, chunk).wait_recv()

            if step < heads - 1:

                @pl.when(within(me - sign * step) & within(me + sign))
                def _():
                    block_copy(side, sign, step, chunk).start()

    if onward:
        own = pltpu.make_async_copy(
            stream_ref, whole_ref.at[:, pl.ds(pl.multiple_of(me * width, width), width)], own_sem
        )

        @pl.when(segment == 0)
        def _():
            own.start()
            own.wait()

    stages = [functools.partial(send_sums, distance) for distance in range(heads - 1, 0, -1)]
    stages.append(finish)
    if onward:
        stages += [functools.partial(send_blocks, step) for step in range(heads)]
    for moment in range(chunks + len(stages) - 1):
        for index, stage in enumerate(stages):
            if 0 <= moment - index < chunks:
                stage(moment - index)

    for chunk in range(chunks):
        for side, sign in sides:
            for distance in range(1, heads):

                @pl.when(within(me + sign * distance))
                def _():
                    sum_copy(side, sign, distance, chunk, True).wait_send()

            if onward:
                for step in range(heads - 1):

                    @pl.when(within(me - sign * step) & within(me + sign))
                    def _():
                        block_copy(side, sign, step, chunk).wait_send()

        if onward:

            @pl.when(segment + 1 < segments)
            def _():
                hop(chunk).wait_send()


def exchange(terms, residual, following):
    heads, rows, width = terms.shape
    segments = lax.axis_size("segment")
    onward = following is not None
    chunks = 4
    vmem = pl.BlockSpec(memory_space=pltpu.VMEM)
    shapes = [jax.ShapeDtypeStruct((rows, width), jnp.bfloat16)]
    scratch = [
        pltpu.VMEM((2, heads, rows, width), jnp.bfloat16),
        pltpu.VMEM((rows // chunks, width), jnp.float32),
    ] + [pltpu.SemaphoreType.DMA((2, heads, chunks))] * 2
    operands = [terms, residual]
    if onward:
        operands.append(following)
        shapes.append(jax.ShapeDtypeStruct((rows, heads * width), jnp.bfloat16))
        scratch += [pltpu.SemaphoreType.DMA((2, heads, chunks))] * 2
        scratch += [pltpu.SemaphoreType.DMA((chunks,))] * 2 + [pltpu.SemaphoreType.DMA]
    return pl.pallas_call(
        functools.partial(exchange_kernel, heads, segments, chunks, onward),
        name="exchange" if onward else "reduce",
        out_shape=tuple(shapes),
        in_specs=[vmem] * len(operands),
        out_specs=(vmem,) * len(shapes),
        scratch_shapes=scratch,
        compiler_params=pltpu.CompilerParams(
            collective_id=1 if onward else 2,
            has_side_effects=True,
            vmem_limit_bytes=24 * 1024 * 1024,
        ),
    )(*operands)


def gather_heads(block):
    heads = lax.axis_size("head")
    spread = jnp.broadcast_to(block[None], (heads,) + block.shape)
    return lax.all_to_all(spread, "head", split_axis=0, concat_axis=0, tiled=True)


def run_section(
    whole, gain_row, qkv_matrix, head_gains, rate_row, out_gain_row, out_weights, fasts, norms, active
):
    rows = whole.shape[0]
    heads = lax.axis_size("head")
    head_width = head_gains.shape[-1]
    normed = (rms_scale(whole.astype(jnp.float32)) * gain_row).astype(jnp.bfloat16)
    projected = dot(normed, qkv_matrix).reshape(rows, 3, head_width)
    queries = (rms_scale(projected[:, 0]) * head_gains[0]).astype(jnp.bfloat16)
    key_rows = (rms_scale(projected[:, 1]) * head_gains[1]).astype(jnp.bfloat16)
    out_grad = (-rate_row[:, None] * projected[:, 2]).astype(jnp.bfloat16)
    both = gather_tokens(jnp.stack([key_rows, out_grad]))
    return fast_step(active, both, queries, fasts, norms, out_gain_row, out_weights, heads)


def shards(stream, in_gain, w_qkv, qk_gain, w_one, w_three, w_two, token_rate, out_gain, w_out):
    segment_index = lax.axis_index("segment")
    span_count = stream.shape[0]
    moments = span_count + lax.axis_size("segment") - 1
    qkv_matrix = w_qkv[0].reshape(w_qkv.shape[1], -1)
    fasts = (
        w_one[0, 0].astype(jnp.float32),
        w_three[0, 0].astype(jnp.float32),
        w_two[0, 0].astype(jnp.float32).T,
    )
    norms = (
        jnp.stack([jnp.sqrt(jnp.sum(matrix * matrix, axis=0, keepdims=True)) for matrix in fasts[:2]]),
        jnp.sqrt(jnp.sum(fasts[2] * fasts[2], axis=1, keepdims=True)),
    )
    collected = jnp.zeros(stream.shape, jnp.bfloat16)
    source = stream[0]
    whole = gather_heads(source).swapaxes(0, 1).reshape(source.shape[0], -1)
    for moment in range(moments):
        span_index = moment - segment_index
        active = (span_index >= 0) & (span_index < span_count)
        clipped = jnp.clip(span_index, 0, span_count - 1)
        rate_row = lax.dynamic_index_in_dim(token_rate[0], clipped, 0, keepdims=False)
        terms, *fasts = run_section(
            whole,
            in_gain[0],
            qkv_matrix,
            qk_gain[0, 0],
            rate_row,
            out_gain[0, :1],
            w_out[0, 0],
            fasts,
            norms,
            active.astype(jnp.int32)[None],
        )
        if moment + 1 < moments:
            following = stream[min(moment + 1, span_count - 1)]
            result, whole = exchange(terms, source, following)
            source = lax.dynamic_slice_in_dim(
                whole, lax.axis_index("head") * source.shape[1], source.shape[1], axis=1
            )
        else:
            (result,) = exchange(terms, source, None)
        chosen = jnp.arange(span_count) == span_index
        collected = jnp.where(chosen[:, None, None], result[None], collected)
    return collected[None]


def solution(mesh):
    placed = (
        P(None, "seq", "head"),
        P("segment", None),
        P("segment", None, "head", None, None),
        P("segment", "head", None, None),
        P("segment", "head", None, None),
        P("segment", "head", None, None),
        P("segment", "head", None, None),
        P("segment", None, "seq"),
        P("segment", "head", None),
        P("segment", "head", None, None),
    )
    return jax.shard_map(
        shards,
        mesh=mesh,
        in_specs=placed,
        out_specs=P("segment", None, "seq", "head"),
        check_vma=False,
    )
```

profile of v0, /device:TPU:3, one launch (start us, length us, event | category | flops | bytes accessed | tf_op | source)
XLA Modules:
  0.0 246.5 jit_solution(12727152949286967580)
XLA Ops:
  0.0 1.1 slice_bitcast_fusion.6
  1.2 1.1 broadcast_in_dim.91
  2.3 4.7 %all-to-all-start = ((bf16[4,128,1024]{2,1,0:T(8,128)(2,1)}), bf16[4,128,1024]{2,1,0:T(8,128)(2,1)}, u32[]{:S(2)}, u32[]{:S(2)}) async-start(bf16[4,128,1024]{2,1,0:T(8,128)(2,1)} %broadcast_in_dim.91), calls=%async_computation | async-start | bytes 2097152 | tf_op jit(solution)/shard_map/all_to_all | solution.py:488
  7.2 0.2 multiply_reduce_fusion.1
  7.4 0.6 broadcast.351
  8.0 0.7 reduce.9
  8.8 1.4 copy.25
  10.2 0.2 multiply_reduce_fusion
  10.6 16.9 %copy.23 = bf16[1,4096,1,3,512]{1,4,3,2,0:T(8,128)(2,1)} copy(bf16[1,4096,1,3,512]{4,1,3,2,0:T(8,128)(2,1)} %param.12) | data formatting | bytes 25165824 | tf_op args[2]
  27.8 0.9 copy-done.9
  28.7 0.2 copy-done.11
  28.9 1.9 bitcast_convert_fusion
  30.8 1.6 all-to-all-done
  32.4 1.6 copy.22
  34.0 0.6 fusion.6
  34.6 0.7 fusion.8
  35.3 9.0 %fusion.4 = f32[128,3,512]{2,0,1:T(8,128)S(1)} fusion(bf16[128,4096,1]{0,1,2:T(8,128)(2,1)S(1)} %bitcast.121, bf16[1,4096,1,3,512]{1,4,3,2,0:T(8,128)(2,1)} %copy.23), kind=kOutput, calls=%fused_computation.4 | convolution fusion | flops 1610612736 | bytes 14417920 | tf_op jit(solution)/shard_map/dot_general | solution.py:26
  44.8 10.9 %gather_tokens.3.both_ref = bf16[2,512,512]{2,1,0:T(8,128)(2,1)S(1)} custom-call(bf16[2,128,512]{2,1,0:T(8,128)(2,1)S(1)} %pad_maximum_fusion.own_ref), custom_call_target="tpu_custom_call" | custom-call | tf_op jit(solution)/shard_map/gather_tokens/pallas_call | solution.py:235
  55.9 18.4 %fast_step.3 = (bf16[4,128,1024]{2,1,0:T(8,128)(2,1)S(1)}, f32[512,768]{1,0:T(8,128)S(1)}, f32[512,768]{1,0:T(8,128)S(1)}, f32[512,768]{1,0:T(8,128)S(1)}) custom-call(s32[1]{0:T(128)} %bitcast.2.active_ref, bf16[2,512,512]{2,1,0:T(8,128)(2,1)S(1)} %gather_tokens.3.both_ref, bf16[128,512]{1,0:T(8,128)(2,1)S(1)} %multiply_convert_fusion.2.query_ref, ...), custom_call_target="tpu_custom_call" | custom-call | flops 10000000000 | bytes 20000000 | tf_op jit(solution)/shard_map/fast_step/pallas_call | solution.py:138
  74.2 1.2 copy-done.6
  75.4 35.7 %exchange.2 = (bf16[128,1024]{1,0:T(8,128)(2,1)S(1)}, bf16[128,4096]{1,0:T(8,128)(2,1)S(1)}) custom-call(bf16[4,128,1024]{2,1,0:T(8,128)(2,1)S(1)} %get-tuple-element.18.refs_0_, bf16[128,1024]{1,0:T(8,128)(2,1)S(1)} %get-tuple-element.38.refs_1_, bf16[128,1024]{1,0:T(8,128)(2,1)S(1)} %get-tuple-element.37.refs_2_), custom_call_target="tpu_custom_call" | custom-call | tf_op jit(solution)/shard_map/exchange/pallas_call | solution.py:470
  111.2 0.3 fusion.9
  111.5 8.9 %fusion.2 = f32[128,3,512]{2,0,1:T(8,128)S(1)} fusion(bf16[1,4096,1,3,512]{1,4,3,2,0:T(8,128)(2,1)} %copy.23, bf16[128,4096]{1,0:T(8,128)(2,1)S(1)} %get-tuple-element.19, f32[4096]{0:T(1024)S(1)} %bitcast.122, f32[128]{0:T(128)S(1)} %add_rsqrt_fusion.5), kind=kOutput, calls=%fused_computation.2 | convolution fusion | flops 1612709888 | bytes 14434816 | tf_op jit(solution)/shard_map/dot_general | solution.py:26
  120.9 10.3 %gather_tokens.4.both_ref = bf16[2,512,512]{2,1,0:T(8,128)(2,1)S(1)} custom-call(bf16[2,128,512]{2,1,0:T(8,128)(2,1)S(1)} %pad_maximum_fusion.1.own_ref), custom_call_target="tpu_custom_call" | custom-call | tf_op jit(solution)/shard_map/gather_tokens/pallas_call | solution.py:235
  131.2 18.4 %fast_step.4 = (bf16[4,128,1024]{2,1,0:T(8,128)(2,1)S(1)}, f32[512,768]{1,0:T(8,128)S(1)}, f32[512,768]{1,0:T(8,128)S(1)}, f32[512,768]{1,0:T(8,128)S(1)}) custom-call(s32[1]{0:T(128)} %bitcast.1.active_ref, bf16[2,512,512]{2,1,0:T(8,128)(2,1)S(1)} %gather_tokens.4.both_ref, bf16[128,512]{1,0:T(8,128)(2,1)S(1)} %multiply_convert_fusion.1.query_ref, ...), custom_call_target="tpu_custom_call" | custom-call | flops 10000000000 | bytes 20000000 | tf_op jit(solution)/shard_map/fast_step/pallas_call | solution.py:138
  149.7 35.8 %exchange.3 = (bf16[128,1024]{1,0:T(8,128)(2,1)S(1)}, bf16[128,4096]{1,0:T(8,128)(2,1)S(1)}) custom-call(bf16[4,128,1024]{2,1,0:T(8,128)(2,1)S(1)} %get-tuple-element.23.refs_0_, bf16[128,1024]{1,0:T(8,128)(2,1)S(1)} %constant_dynamic-slice_fusion.2.refs_1_, bf16[128,1024]{1,0:T(8,128)(2,1)S(1)} %get-tuple-element.37.refs_2_), custom_call_target="tpu_custom_call" | custom-call | tf_op jit(solution)/shard_map/exchange/pallas_call | solution.py:470
  185.5 0.3 fusion.12
  185.8 8.9 %fusion = f32[128,3,512]{2,0,1:T(8,128)S(1)} fusion(bf16[1,4096,1,3,512]{1,4,3,2,0:T(8,128)(2,1)} %copy.23, bf16[128,4096]{1,0:T(8,128)(2,1)S(1)} %get-tuple-element.24, f32[128]{0:T(128)S(1)} %add_rsqrt_fusion.2, f32[4096]{0:T(1024)S(1)} %bitcast.123), kind=kOutput, calls=%fused_computation | convolution fusion | flops 1612709888 | bytes 14434816 | tf_op jit(solution)/shard_map/dot_general | solution.py:26
  195.2 11.3 %gather_tokens.5.both_ref = bf16[2,512,512]{2,1,0:T(8,128)(2,1)S(1)} custom-call(bf16[2,128,512]{2,1,0:T(8,128)(2,1)S(1)} %pad_maximum_fusion.2.own_ref), custom_call_target="tpu_custom_call" | custom-call | tf_op jit(solution)/shard_map/gather_tokens/pallas_call | solution.py:235
  206.5 20.1 %fast_step.5 = (bf16[4,128,1024]{2,1,0:T(8,128)(2,1)S(1)}, f32[512,768]{1,0:T(8,128)}, f32[512,768]{1,0:T(8,128)}, f32[512,768]{1,0:T(8,128)}) custom-call(s32[1]{0:T(128)} %bitcast.active_ref, bf16[2,512,512]{2,1,0:T(8,128)(2,1)S(1)} %gather_tokens.5.both_ref, bf16[128,512]{1,0:T(8,128)(2,1)S(1)} %multiply_convert_fusion.query_ref, ...), custom_call_target="tpu_custom_call" | custom-call | flops 10000000000 | bytes 20000000 | tf_op jit(solution)/shard_map/fast_step/pallas_call | solution.py:138
  226.7 18.8 %reduce.10 = bf16[128,1024]{1,0:T(8,128)(2,1)S(1)} custom-call(bf16[4,128,1024]{2,1,0:T(8,128)(2,1)S(1)} %get-tuple-element.28.refs_0_, bf16[128,1024]{1,0:T(8,128)(2,1)S(1)} %constant_dynamic-slice_fusion.refs_1_), custom_call_target="tpu_custom_call" | custom-call | tf_op jit(solution)/shard_map/reduce/pallas_call | solution.py:470
  245.5 0.9 select_select_fusion
  (66 shorter events, 2.0 us)
Async XLA Ops:
  0.0 7.0 %copy-start.10 = (bf16[1,1,512,768]{3,2,1,0:T(8,128)(2,1)S(1)}, bf16[1,1,512,768]{3,2,1,0:T(8,128)(2,1)}, u32[]{:S(2)}) copy-start(bf16[1,1,512,768]{3,2,1,0:T(8,128)(2,1)} %param.14) | copy-start | bytes 2359300
  1.1 6.1 %copy-start.8 = (bf16[1,1,512,768]{3,2,1,0:T(8,128)(2,1)S(1)}, bf16[1,1,512,768]{3,2,1,0:T(8,128)(2,1)}, u32[]{:S(2)}) copy-start(bf16[1,1,512,768]{3,2,1,0:T(8,128)(2,1)} %param.15) | copy-start | bytes 2359300
  2.3 5.7 %copy-start.12 = (f32[1,4096]{1,0:T(1,128)S(1)}, f32[1,4096]{1,0:T(1,128)}, u32[]{:S(2)}) copy-start(f32[1,4096]{1,0:T(1,128)} %param.11) | copy-start | bytes 49156
  2.3 30.1 %all-to-all-start = ((bf16[4,128,1024]{2,1,0:T(8,128)(2,1)}), bf16[4,128,1024]{2,1,0:T(8,128)(2,1)}, u32[]{:S(2)}, u32[]{:S(2)}) async-start(bf16[4,128,1024]{2,1,0:T(8,128)(2,1)} %broadcast_in_dim.91), calls=%async_computation | async-start | bytes 2097152 | tf_op jit(solution)/shard_map/all_to_all | solution.py:488
  10.6 17.0 %copy-start.14 = (f32[1,2,128]{2,1,0:T(2,128)S(1)}, f32[1,2,128]{2,1,0:T(2,128)}, u32[]{:S(2)}) copy-start(f32[1,2,128]{2,1,0:T(2,128)} %param.17) | copy-start | bytes 3076
  10.6 17.0 %copy-start.13 = (f32[1,1,2,512]{3,2,1,0:T(2,128)S(1)}, f32[1,1,2,512]{3,2,1,0:T(2,128)}, u32[]{:S(2)}) copy-start(f32[1,1,2,512]{3,2,1,0:T(2,128)} %param.13) | copy-start | bytes 12292
  27.5 1.1 copy-start.9
  27.5 1.4 copy-start.11
  35.3 20.5 %copy-start.2 = (bf16[1,1,512,4096]{3,2,1,0:T(8,128)(2,1)S(1)}, bf16[1,1,512,4096]{3,2,1,0:T(8,128)(2,1)}, u32[]{:S(2)}) copy-start(bf16[1,1,512,4096]{3,2,1,0:T(8,128)(2,1)} %param.19) | copy-start | bytes 12582916
  44.3 11.5 %copy-start = (f32[512,768]{1,0:T(8,128)S(1)}, f32[512,768]{1,0:T(8,128)}, u32[]{:S(2)}) copy-start(f32[512,768]{1,0:T(8,128)} %get-tuple-element.44.up_ref) | copy-start | bytes 4718596
  44.4 11.5 %copy-start.1 = (f32[512,768]{1,0:T(8,128)S(1)}, f32[512,768]{1,0:T(8,128)}, u32[]{:S(2)}) copy-start(f32[512,768]{1,0:T(8,128)} %get-tuple-element.45.gate_ref) | copy-start | bytes 4718596
  44.4 11.5 %copy-start.3 = (f32[1,1,512]{2,1,0:T(1,128)S(1)}, f32[1,1,512]{2,1,0:T(1,128)}, u32[]{:S(2)}) copy-start(f32[1,1,512]{2,1,0:T(1,128)} %param.18) | copy-start | bytes 6148
  74.2 1.2 copy-start.6
  75.4 35.7 %copy-start.4 = (f32[512,768]{1,0:T(8,128)}, f32[512,768]{1,0:T(8,128)S(1)}, u32[]{:S(2)}) copy-start(f32[512,768]{1,0:T(8,128)S(1)} %get-tuple-element.21.up_ref) | copy-start | bytes 4718596
  120.3 10.9 %copy-start.5 = (f32[512,768]{1,0:T(8,128)S(1)}, f32[512,768]{1,0:T(8,128)}, u32[]{:S(2)}) copy-start(f32[512,768]{1,0:T(8,128)} %copy-done.4) | copy-start | bytes 4718596
  120.4 10.9 %copy-start.7 = (f32[512,768]{1,0:T(8,128)S(1)}, f32[512,768]{1,0:T(8,128)}, u32[]{:S(2)}) copy-start(f32[512,768]{1,0:T(8,128)} %copy-done.6) | copy-start | bytes 4718596
where the time goes:
time: 251 us; the launch traced here: 246 us
  Pallas kernels  180 us (72%)
  matrix products  26.8 us (11%)
  local copies, waits for them, and re-layouts  25.5 us (10%)
  other arithmetic  7.55 us (3%)
  starting transfers between devices  4.72 us (2%)
    pallas_call x3, Pallas kernels, exchange(): pl.pallas_call(functools.partial(exchange_kernel, heads, segments, chunks...  90.3 us
    pallas_call x3, Pallas kernels, fast_step(): pl.pallas_call(fast_kernel, name='fast_step', out_shape=(jax.ShapeDtypeSt...  56.9 us
    pallas_call x3, Pallas kernels, gather_tokens(): pl.pallas_call(functools.partial(gather_tokens_kernel, devices), name='ga...  32.6 us
    dot_general x3, matrix products, dot(): return jnp.dot(left, right, preferred_element_type=jnp.float32)  26.8 us
    unnamed x34, local copies, waits for them, and re-layouts  21.3 us
  transfers between devices with their start and end apart: 1, of which 1 were waited for; matrix products, arithmetic and copies ran while one was open for 9% of the time, Pallas kernels for 0%

commit v1 on v0

v1 whole, which is shorter than its diff:
```python
import functools

import jax
import jax.numpy as jnp
from jax import lax
from jax.experimental import pallas as pl
from jax.experimental.pallas import tpu as pltpu
from jax.sharding import PartitionSpec as P

NS_STEPS = 2

ns_first = 3.4445
ns_second = -4.775
ns_third = 2.0315
update_step = 1.0
norm_eps = 1e-06
grad_eps = 1e-07


def rms_scale(values):
    return values * lax.rsqrt(jnp.mean(values * values, axis=-1, keepdims=True) + norm_eps)


def dot(left, right):
    return jnp.dot(left, right, preferred_element_type=jnp.float32)


def contract(left, right, dims):
    return lax.dot_general(
        left, right, ((dims[:1], dims[1:]), ((), ())), preferred_element_type=jnp.float32
    )


def signal(semaphore, target):
    pl.semaphore_signal(
        semaphore, inc=1, device_id=target, device_id_type=pl.DeviceIdType.MESH
    )


def remote(source, target, send_sem, recv_sem, device):
    return pltpu.make_async_remote_copy(
        src_ref=source,
        dst_ref=target,
        send_sem=send_sem,
        recv_sem=recv_sem,
        device_id=device,
        device_id_type=pl.DeviceIdType.MESH,
    )


def step_kernel(
    segments,
    devices,
    heads,
    chunks,
    stream_hbm,
    in_gain_ref,
    qkv_hbm,
    qk_gain_ref,
    gate_hbm,
    up_hbm,
    down_hbm,
    rate_ref,
    out_gain_ref,
    out_hbm,
    result_ref,
    qkv,
    out_weights,
    wide_init,
    down_init,
    whole,
    scaled,
    sums,
    both,
    queries,
    rights,
    work,
    state,
    wide_norms,
    down_norm,
    terms,
    slots,
    qkv_sems,
    load_sems,
    own_sems,
    spread_sends,
    arrivals,
    far_sends,
    far_recvs,
    near_sends,
    near_recvs,
    term_sends,
    term_recvs,
    hop_sends,
    relay_sends,
):
    segment = lax.axis_index("segment")
    place_seq = lax.axis_index("seq")
    me = lax.axis_index("head")
    spans, rows, width = result_ref.shape
    features = whole.shape[2]
    chips = devices // 2
    chip, core = place_seq // 2, lax.rem(place_seq, 2)
    partner = {"seq": 2 * chip + 1 - core}
    piece = rows // chunks
    last_segment = segments - 1

    loads = [pltpu.make_async_copy(qkv_hbm.at[part], qkv.at[part], qkv_sems.at[part]) for part in range(3)]
    for part in (1, 2, 0):
        loads[part].start()
    fast_loads = [
        pltpu.make_async_copy(gate_hbm, wide_init.at[0], load_sems.at[0]),
        pltpu.make_async_copy(up_hbm, wide_init.at[1], load_sems.at[1]),
        pltpu.make_async_copy(down_hbm, down_init, load_sems.at[2]),
    ]
    out_load = pltpu.make_async_copy(out_hbm, out_weights, load_sems.at[3])
    for copy in fast_loads + [out_load]:
        copy.start()

    def other_head(step):
        return lax.rem(me + step, heads)

    barrier = pltpu.get_barrier_semaphore()
    for away in range(segments):
        for step in range(heads):
            if away or step:
                signal(barrier, {"segment": lax.rem(segment + away, segments), "head": other_head(step)})
    for step in range(1, chips):
        signal(barrier, {"seq": 2 * lax.rem(chip + step, chips) + core})
    signal(barrier, partner)
    pl.semaphore_wait(barrier, segments * heads - 1 + chips)

    def columns_of(origin):
        return pl.ds(pl.multiple_of(origin * width, width), width)

    def rows_of(chunk):
        if isinstance(chunk, int):
            return pl.ds(chunk * piece, piece)
        return pl.ds(pl.multiple_of(chunk * piece, piece), piece)

    def place(span, origin, chunk):
        return whole.at[span, rows_of(chunk), columns_of(origin)]

    def spread(span, step, chunk):
        return remote(
            stream_hbm.at[span, rows_of(chunk), :],
            place(span, me, chunk),
            spread_sends.at[span, step, chunk],
            arrivals.at[span, me, chunk],
            {"segment": 0, "head": other_head(step)},
        )

    def each_spread(action):
        for span in range(spans):
            for chunk in range(chunks):

                @pl.when(segment == chunk * segments // chunks)
                def _():
                    for step in range(1, heads):
                        action(spread(span, step, chunk))

    each_spread(lambda copy: copy.start())

    def own_copy(span):
        return pltpu.make_async_copy(
            stream_hbm.at[span], whole.at[span, :, columns_of(me)], own_sems.at[span]
        )

    @pl.when(segment == 0)
    def _():
        for span in range(spans):
            own_copy(span).start()

    for copy in fast_loads:
        copy.wait()
    for index in range(2):
        work[index] = wide_init[index]
        wide = wide_init[index].astype(jnp.float32)
        state[index] = wide
        wide_norms[index] = jnp.sqrt(jnp.sum(wide * wide, axis=0, keepdims=True))
    down = down_init[...].T
    work[2] = down
    down = down.astype(jnp.float32)
    state[2] = down
    down_norm[...] = jnp.sqrt(jnp.sum(down * down, axis=1, keepdims=True))

    def arrival(span, origin, chunk):
        return remote(
            place(span, origin, chunk),
            place(span, origin, chunk),
            hop_sends.at[span, chunk],
            arrivals.at[span, origin, chunk],
            {"head": other_head(1)},
        )

    def relay_copy(span, step, chunk):
        return remote(
            place(span, me, chunk),
            place(span, me, chunk),
            relay_sends.at[span, step, chunk],
            arrivals.at[span, me, chunk],
            {"head": other_head(step)},
        )

    def relay(span, chunk):
        arrival(span, me, chunk).wait_recv()
        for step in range(1, heads):
            relay_copy(span, step, chunk).start()

    def project_keys(span):
        sums[0] = jnp.zeros(sums.shape[1:], jnp.float32)
        sums[1] = jnp.zeros(sums.shape[1:], jnp.float32)

        def block(step, squares):
            origin = other_head(step)

            @pl.when(step > 0)
            def _():
                for chunk in range(chunks):
                    arrival(span, origin, chunk).wait_recv()

            here = columns_of(origin)
            values = whole[span, :, here].astype(jnp.float32)
            scaled[:, here] = (values * in_gain_ref[:, here]).astype(jnp.bfloat16)
            sums[0] += dot(scaled[:, here], qkv[1, here, :])
            sums[1] += dot(scaled[:, here], qkv[2, here, :])
            return squares + jnp.sum(values * values, axis=1, keepdims=True)

        squares = lax.fori_loop(0, heads, block, jnp.zeros((rows, 1), jnp.float32))
        return lax.rsqrt(squares * (1.0 / features) + norm_eps)

    def rows_at(origin, count=1):
        return pl.ds(pl.multiple_of(origin * rows, rows), count * rows)

    def far_copy(span, part, step):
        return remote(
            both.at[span, part, rows_at(place_seq), :],
            both.at[span, part, rows_at(place_seq), :],
            far_sends.at[span, part, step],
            far_recvs.at[span, part, step],
            {"seq": 2 * lax.rem(chip + step, chips) + core},
        )

    def near_copy(span, part, step):
        origin = 2 * lax.rem(chip + chips - step, chips) + core
        return remote(
            both.at[span, part, rows_at(origin), :],
            both.at[span, part, rows_at(origin), :],
            near_sends.at[span, part, step],
            near_recvs.at[span, part, step],
            partner,
        )

    def project(span):
        scale = project_keys(span)
        own = rows_at(place_seq)
        both[span, 0, own, :] = (rms_scale(sums[0] * scale) * qk_gain_ref[1:2, :]).astype(jnp.bfloat16)
        diagonal = lax.broadcasted_iota(jnp.int32, (rows, rows), 0) == lax.broadcasted_iota(
            jnp.int32, (rows, rows), 1
        )
        rates = jnp.sum(
            jnp.where(diagonal, rate_ref[pl.ds(span, 1), :], 0.0), axis=1, keepdims=True
        )
        both[span, 1, own, :] = (-rates * (sums[1] * scale)).astype(jnp.bfloat16)
        for part in range(2):
            for step in range(1, chips):
                far_copy(span, part, step).start()
        for part in range(2):
            near_copy(span, part, 0).start()
        sums[0] = dot(scaled[...], qkv[0])
        queries[...] = (rms_scale(sums[0] * scale) * qk_gain_ref[0:1, :]).astype(jnp.bfloat16)

    def finish(span, chunk):
        here = rows_of(chunk)
        total = whole[span, here, columns_of(me)].astype(jnp.float32) + terms[
            span, me, here, :
        ].astype(jnp.float32)
        for step in range(1, heads):
            origin = other_head(step)
            term_arrival(span, origin, chunk).wait_recv()
            total += slots[span, origin, here, :].astype(jnp.float32)
        result_ref[span, here, :] = total.astype(jnp.bfloat16)

        @pl.when(segment < last_segment)
        def _():
            hop(span, chunk).start()

    def term_copy(span, step, chunk):
        target = other_head(step)
        return remote(
            terms.at[span, target, rows_of(chunk), :],
            slots.at[span, me, rows_of(chunk), :],
            term_sends.at[span, step, chunk],
            term_recvs.at[span, me, chunk],
            {"head": target},
        )

    def term_arrival(span, origin, chunk):
        return remote(
            slots.at[span, origin, rows_of(chunk), :],
            slots.at[span, origin, rows_of(chunk), :],
            hop_sends.at[span, chunk],
            term_recvs.at[span, origin, chunk],
            {"head": other_head(1)},
        )

    def hop(span, chunk):
        return remote(
            result_ref.at[span, rows_of(chunk), :],
            place(span, me, chunk),
            hop_sends.at[span, chunk],
            arrivals.at[span, me, chunk],
            {"segment": segment + 1},
        )

    def between(span, chunk):
        @pl.when(span > 0)
        def _():
            finish(span - 1, chunk)

        @pl.when((segment > 0) & (span + 1 < spans))
        def _():
            relay(span + 1, chunk)

    def gradients(span, step):
        for part in range(2):

            @pl.when(step > 0)
            def _():
                remote(
                    both.at[span, part, rows_at(2 * lax.rem(chip + chips - step, chips) + core), :],
                    both.at[span, part, rows_at(2 * lax.rem(chip + chips - step, chips) + core), :],
                    far_sends.at[span, part, step],
                    far_recvs.at[span, part, step],
                    partner,
                ).wait_recv()
                near_copy(span, part, step).start()

        origin = lax.rem(chip + chips - step, chips)
        for part in range(2):
            twin = rows_at(2 * origin + 1 - core)
            remote(
                both.at[span, part, twin, :],
                both.at[span, part, twin, :],
                near_sends.at[span, part, step],
                near_recvs.at[span, part, step],
                partner,
            ).wait_recv()
        here = rows_at(2 * origin, 2)
        keys = both[span, 0, here, :]
        grads = both[span, 1, here, :]
        pre_gate = dot(keys, work[0])
        pre_up = dot(keys, work[1])
        backward = dot(grads, work[2])
        sigmoid_gate = jax.nn.sigmoid(pre_gate)
        gated = pre_gate * sigmoid_gate
        rights[0, here, :] = (
            backward * pre_up * sigmoid_gate * (1.0 + pre_gate * (1.0 - sigmoid_gate))
        ).astype(jnp.bfloat16)
        rights[1, here, :] = (backward * gated).astype(jnp.bfloat16)
        rights[2, here, :] = (gated * pre_up).astype(jnp.bfloat16)

    def orthogonalize(span, index):
        gradient = contract(both[span, index // 2], rights[index], (0, 0))
        scale = 1.0 / (jnp.sqrt(jnp.sum(gradient * gradient, keepdims=True)) + grad_eps)
        work[index] = (gradient * scale).astype(jnp.bfloat16)

        def sweep(step, inner):
            current = work[index]
            gram_matrix = contract(current, current, (1, 1)).astype(jnp.bfloat16)
            square = dot(gram_matrix, gram_matrix)
            mixing = (ns_second * gram_matrix.astype(jnp.float32) + ns_third * square).astype(
                jnp.bfloat16
            )
            work[index] = (ns_first * current.astype(jnp.float32) + dot(mixing, current)).astype(
                jnp.bfloat16
            )
            return inner

        lax.fori_loop(0, NS_STEPS, sweep, 0)

    def update():
        for index, axis, target in (
            (0, 0, wide_norms[0]),
            (1, 0, wide_norms[1]),
            (2, 1, down_norm[...]),
        ):
            moved = state[index] - update_step * work[index].astype(jnp.float32)
            length = jnp.sqrt(jnp.sum(moved * moved, axis=axis, keepdims=True)) + norm_eps
            fresh = moved * (target / length)
            work[index] = fresh.astype(jnp.bfloat16)
            state[index] = fresh

    def read_out(span):
        gate_out = dot(queries[...], work[0])
        up_out = dot(queries[...], work[1])
        inner = (gate_out * jax.nn.sigmoid(gate_out) * up_out).astype(jnp.bfloat16)
        output = contract(inner, work[2], (1, 1))
        normed_out = (rms_scale(output) * out_gain_ref[...]).astype(jnp.bfloat16)

        def term(origin, carry):
            terms[span, origin] = dot(normed_out, out_weights[:, columns_of(origin)]).astype(
                jnp.bfloat16
            )
            return carry

        lax.fori_loop(0, heads, term, 0)
        for chunk in range(chunks):
            for step in range(1, heads):
                term_copy(span, step, chunk).start()

    @pl.when(segment == 0)
    def _():
        for span in range(spans):
            own_copy(span).wait()

    @pl.when(segment > 0)
    def _():
        for chunk in range(chunks):
            relay(0, chunk)

    for part in (1, 2, 0):
        loads[part].wait()
    out_load.wait()

    def block(span, carry):
        project(span)

        def gradient_step(step, inner):
            gradients(span, step)
            return inner

        lax.fori_loop(0, chips, gradient_step, 0)
        between(span, 0)

        def orthogonal_step(index, inner):
            orthogonalize(span, index)

            @pl.when(index + 1 < chunks)
            def _():
                between(span, index + 1)

            return inner

        lax.fori_loop(0, 3, orthogonal_step, 0)
        update()
        read_out(span)
        return carry

    lax.fori_loop(0, spans, block, 0)
    for chunk in range(chunks):
        finish(spans - 1, chunk)

    each_spread(lambda copy: copy.wait_send())

    def drain(span, carry):
        for chunk in range(chunks):
            for step in range(1, heads):
                term_copy(span, step, chunk).wait_send()

            @pl.when(segment > 0)
            def _():
                for step in range(1, heads):
                    relay_copy(span, step, chunk).wait_send()

            @pl.when(segment < last_segment)
            def _():
                hop(span, chunk).wait_send()

        for part in range(2):
            for step in range(1, chips):
                far_copy(span, part, step).wait_send()
            for step in range(chips):
                near_copy(span, part, step).wait_send()
        return carry

    lax.fori_loop(0, spans, drain, 0)


def shards(stream, in_gain, w_qkv, qk_gain, w_one, w_three, w_two, token_rate, out_gain, w_out):
    segments = lax.axis_size("segment")
    devices = lax.axis_size("seq")
    heads = lax.axis_size("head")
    spans, rows, width = stream.shape
    features = w_qkv.shape[1]
    inner, wide = w_one.shape[2:]
    tokens = devices * rows
    chunks = 4
    vmem = pl.BlockSpec(memory_space=pltpu.VMEM)
    anywhere = pl.BlockSpec(memory_space=pl.ANY)
    low = jnp.bfloat16
    dma = pltpu.SemaphoreType.DMA
    result = pl.pallas_call(
        functools.partial(step_kernel, segments, devices, heads, chunks),
        name="step",
        out_shape=jax.ShapeDtypeStruct(stream.shape, low),
        in_specs=[anywhere, vmem, anywhere, vmem, anywhere, anywhere, anywhere, vmem, vmem, anywhere],
        out_specs=vmem,
        scratch_shapes=[
            pltpu.VMEM((3, features, inner), low),
            pltpu.VMEM((inner, features), low),
            pltpu.VMEM((2, inner, wide), low),
            pltpu.VMEM((wide, inner), low),
            pltpu.VMEM((spans, rows, features), low),
            pltpu.VMEM((rows, features), low),
            pltpu.VMEM((2, rows, inner), jnp.float32),
            pltpu.VMEM((spans, 2, tokens, inner), low),
            pltpu.VMEM((rows, inner), low),
            pltpu.VMEM((3, tokens, wide), low),
            pltpu.VMEM((3, inner, wide), low),
            pltpu.VMEM((3, inner, wide), jnp.float32),
            pltpu.VMEM((2, 1, wide), jnp.float32),
            pltpu.VMEM((inner, 1), jnp.float32),
            pltpu.VMEM((spans, heads, rows, width), low),
            pltpu.VMEM((spans, heads, rows, width), low),
            dma((3,)),
            dma((4,)),
            dma((spans,)),
            dma((spans, heads, chunks)),
            dma((spans, heads, chunks)),
            dma((spans, 2, devices // 2)),
            dma((spans, 2, devices // 2)),
            dma((spans, 2, devices // 2)),
            dma((spans, 2, devices // 2)),
            dma((spans, heads, chunks)),
            dma((spans, heads, chunks)),
            dma((spans, chunks)),
            dma((spans, heads, chunks)),
        ],
        compiler_params=pltpu.CompilerParams(
            collective_id=0, has_side_effects=True, vmem_limit_bytes=67043328
        ),
    )(
        stream,
        in_gain,
        jnp.transpose(w_qkv[0, :, 0], (1, 0, 2)),
        qk_gain[0, 0],
        w_one[0, 0],
        w_three[0, 0],
        w_two[0, 0],
        token_rate[0],
        out_gain[0, :1],
        w_out[0, 0],
    )
    return result[None]


def solution(mesh):
    placed = (
        P(None, "seq", "head"),
        P("segment", None),
        P("segment", None, "head", None, None),
        P("segment", "head", None, None),
        P("segment", "head", None, None),
        P("segment", "head", None, None),
        P("segment", "head", None, None),
        P("segment", None, "seq"),
        P("segment", "head", None),
        P("segment", "head", None, None),
    )
    return jax.shard_map(
        shards,
        mesh=mesh,
        in_specs=placed,
        out_specs=P("segment", None, "seq", "head"),
        check_vma=False,
    )
```

time: 251 us -> 184 us (0.73); the launches traced: 246 us -> 184 us
  matrix products: 26.8 us -> 0 us
  local copies, waits for them, and re-layouts: 25.5 us -> 1.87 us
  other arithmetic: 7.55 us -> 0 us
  starting transfers between devices: 4.72 us -> 0 us
    dot_general x3 -> x0, matrix products: 26.8 us -> none  [dot(): return jnp.dot(left, right, preferred_element_type=jnp.float32)]
    unnamed x34 -> x1, local copies, waits for them, and re-layouts: 21.3 us -> 1.87 us
    all_to_all x1 -> x0, starting transfers between devices: 4.72 us -> none  [gather_heads(): lax.all_to_all(spread, 'head', split_axis=0, concat_axis=0, tiled=True)]
    convert_element_type x8 -> x0, other arithmetic: 3.2 us -> none  [the longest x1 1.91 us: shards(): w_three[0, 0].astype(jnp.float32)]
    pallas_call x9 -> x1, Pallas kernels: 180 us -> 182 us  [shards(): pl.pallas_call(functools.partial(step_kernel, segments, devices, heads, c...]
  transfers between devices with their start and end apart: 1 -> 0, of which waited for: 1 -> 0; matrix products, arithmetic and copies ran while one was open for 9% -> 0% of each run, Pallas kernels for 0% -> 0%
where the time goes in v1:
time: 184 us
  Pallas kernels  182 us (99%)
  local copies, waits for them, and re-layouts  1.87 us (1%)
    pallas_call x1, Pallas kernels, shards(): pl.pallas_call(functools.partial(step_kernel, segments, devices, heads, c...  182 us

profile of v1, /device:TPU:3, one launch (start us, length us, event | category | flops | bytes accessed | tf_op | source)
XLA Modules:
  0.0 183.7 jit_solution(5327569834194674261)
XLA Ops:
  0.0 181.8 %step.1 = bf16[2,128,1024]{2,1,0:T(8,128)(2,1)} custom-call(bf16[2,128,1024]{2,1,0:T(8,128)(2,1)} %stream_hbm.1, f32[1,4096]{1,0:T(1,128)} %in_gain_ref.1, bf16[3,4096,512]{2,1,0:T(8,128)(2,1)} %bitcast.11, f32[2,512]{1,0:T(2,128)} %bitcast.17, bf16[512,768]{1,0:T(8,128)(2,1)} %bitcast.14, bf16[512,768]{1,0:T(8,128)(2,1)} %bitcast.15, ...), custom_call_target="tpu_custom_call" | custom-call | tf_op jit(solution)/shard_map/step/pallas_call | solution.py:493
  181.9 1.9 %copy.12 = bf16[1,2,128,1024]{3,2,1,0:T(8,128)(2,1)} copy(bf16[1,2,128,1024]{3,2,1,0:T(8,128)(2,1)} %bitcast.13) | data formatting | bytes 1048576

commit v2 on v1

--- a/solution.py
+++ b/solution.py
@@ -93,6 +93,10 @@
     term_recvs,
     hop_sends,
     relay_sends,
+    around_sends,
+    around_recvs,
+    ready,
+    *vias,
 ):
     segment = lax.axis_index("segment")
     place_seq = lax.axis_index("seq")
@@ -103,18 +107,20 @@
     chip, core = place_seq // 2, lax.rem(place_seq, 2)
     partner = {"seq": 2 * chip + 1 - core}
     piece = rows // chunks
+    unit = chunks // 8
+    around = 4 * unit if segments > 1 else 0
+    via = vias[0] if around else None
     last_segment = segments - 1
+    straight = chunks - 1
 
     loads = [pltpu.make_async_copy(qkv_hbm.at[part], qkv.at[part], qkv_sems.at[part]) for part in range(3)]
-    for part in (1, 2, 0):
-        loads[part].start()
     fast_loads = [
         pltpu.make_async_copy(gate_hbm, wide_init.at[0], load_sems.at[0]),
         pltpu.make_async_copy(up_hbm, wide_init.at[1], load_sems.at[1]),
         pltpu.make_async_copy(down_hbm, down_init, load_sems.at[2]),
     ]
     out_load = pltpu.make_async_copy(out_hbm, out_weights, load_sems.at[3])
-    for copy in fast_loads + [out_load]:
+    for copy in fast_loads:
         copy.start()
 
     def other_head(step):
@@ -150,16 +156,26 @@
             {"segment": 0, "head": other_head(step)},
         )
 
-    def each_spread(action):
-        for span in range(spans):
-            for chunk in range(chunks):
-
-                @pl.when(segment == chunk * segments // chunks)
-                def _():
-                    for step in range(1, heads):
-                        action(spread(span, step, chunk))
-
-    each_spread(lambda copy: copy.start())
+    def each_spread(span, action):
+        share = chunks // segments
+
+        def one(index, carry):
+            for step in range(1, heads):
+                action(spread(span, step, segment * share + index))
+            return carry
+
+        lax.fori_loop(0, share, one, 0)
+
+    def start(copy):
+        copy.start()
+
+    def wait_send(copy):
+        copy.wait_send()
+
+    each_spread(0, start)
+    for part in (1, 2, 0):
+        loads[part].start()
+    out_load.start()
 
     def own_copy(span):
         return pltpu.make_async_copy(
@@ -188,7 +204,7 @@
         return remote(
             place(span, origin, chunk),
             place(span, origin, chunk),
-            hop_sends.at[span, chunk],
+            hop_sends.at[span, 0, chunk],
             arrivals.at[span, origin, chunk],
             {"head": other_head(1)},
         )
@@ -204,8 +220,11 @@
 
     def relay(span, chunk):
         arrival(span, me, chunk).wait_recv()
-        for step in range(1, heads):
-            relay_copy(span, step, chunk).start()
+
+        @pl.when(chunk < straight)
+        def _():
+            for step in range(1, heads):
+                relay_copy(span, step, chunk).start()
 
     def project_keys(span):
         sums[0] = jnp.zeros(sums.shape[1:], jnp.float32)
@@ -216,8 +235,11 @@
 
             @pl.when(step > 0)
             def _():
-                for chunk in range(chunks):
+                def wait(chunk, carry):
                     arrival(span, origin, chunk).wait_recv()
+                    return carry
+
+                lax.fori_loop(0, chunks, wait, 0)
 
             here = columns_of(origin)
             values = whole[span, :, here].astype(jnp.float32)
@@ -283,7 +305,12 @@
 
         @pl.when(segment < last_segment)
         def _():
-            hop(span, chunk).start()
+            hop(span, 0, chunk).start()
+
+            @pl.when(chunk >= straight)
+            def _():
+                for step in range(1, heads):
+                    hop(span, step, chunk).start()
 
     def term_copy(span, step, chunk):
         target = other_head(step)
@@ -299,28 +326,36 @@
         return remote(
             slots.at[span, origin, rows_of(chunk), :],
             slots.at[span, origin, rows_of(chunk), :],
-            hop_sends.at[span, chunk],
+            hop_sends.at[span, 0, chunk],
             term_recvs.at[span, origin, chunk],
             {"head": other_head(1)},
         )
 
-    def hop(span, chunk):
+    def hop(span, step, chunk):
         return remote(
             result_ref.at[span, rows_of(chunk), :],
             place(span, me, chunk),
-            hop_sends.at[span, chunk],
+            hop_sends.at[span, step, chunk],
             arrivals.at[span, me, chunk],
-            {"segment": segment + 1},
-        )
-
-    def between(span, chunk):
+            {"segment": segment + 1, "head": other_head(step)},
+        )
+
+    def between(span, first, count):
         @pl.when(span > 0)
         def _():
-            finish(span - 1, chunk)
+            def one(index, carry):
+                finish(span - 1, first + index)
+                return carry
+
+            lax.fori_loop(0, count, one, 0)
 
         @pl.when((segment > 0) & (span + 1 < spans))
         def _():
-            relay(span + 1, chunk)
+            def one(index, carry):
+                relay(span + 1, first + index)
+                return carry
+
+            lax.fori_loop(0, count, one, 0)
 
     def gradients(span, step):
         for part in range(2):
@@ -360,21 +395,29 @@
         rights[1, here, :] = (backward * gated).astype(jnp.bfloat16)
         rights[2, here, :] = (gated * pre_up).astype(jnp.bfloat16)
 
-    def orthogonalize(span, index):
-        gradient = contract(both[span, index // 2], rights[index], (0, 0))
-        scale = 1.0 / (jnp.sqrt(jnp.sum(gradient * gradient, keepdims=True)) + grad_eps)
-        work[index] = (gradient * scale).astype(jnp.bfloat16)
+    def orthogonalize(span):
+        raw = [contract(both[span, index // 2], rights[index], (0, 0)) for index in range(3)]
+        scales = [
+            1.0 / (jnp.sqrt(jnp.sum(gradient * gradient, keepdims=True)) + grad_eps)
+            for gradient in raw
+        ]
+        for index in range(3):
+            work[index] = (raw[index] * scales[index]).astype(jnp.bfloat16)
 
         def sweep(step, inner):
-            current = work[index]
-            gram_matrix = contract(current, current, (1, 1)).astype(jnp.bfloat16)
-            square = dot(gram_matrix, gram_matrix)
-            mixing = (ns_second * gram_matrix.astype(jnp.float32) + ns_third * square).astype(
-                jnp.bfloat16
-            )
-            work[index] = (ns_first * current.astype(jnp.float32) + dot(mixing, current)).astype(
-                jnp.bfloat16
-            )
+            between(span, (3 + step) * unit, unit)
+            current = [work[index] for index in range(3)]
+            grams = [contract(matrix, matrix, (1, 1)).astype(jnp.bfloat16) for matrix in current]
+            squares = [dot(gram, gram) for gram in grams]
+            mixings = [
+                (ns_second * gram.astype(jnp.float32) + ns_third * square).astype(jnp.bfloat16)
+                for gram, square in zip(grams, squares)
+            ]
+            for index in range(3):
+                work[index] = (
+                    ns_first * current[index].astype(jnp.float32)
+                    + dot(mixings[index], current[index])
+                ).astype(jnp.bfloat16)
             return inner
 
         lax.fori_loop(0, NS_STEPS, sweep, 0)
@@ -398,16 +441,66 @@
         output = contract(inner, work[2], (1, 1))
         normed_out = (rms_scale(output) * out_gain_ref[...]).astype(jnp.bfloat16)
 
-        def term(origin, carry):
-            terms[span, origin] = dot(normed_out, out_weights[:, columns_of(origin)]).astype(
-                jnp.bfloat16
-            )
+        for origin in range(heads):
+            terms[span, origin] = dot(
+                normed_out, out_weights[:, origin * width : (origin + 1) * width]
+            ).astype(jnp.bfloat16)
+    def detours(span, chunk):
+        return (segment == last_segment) & (span == spans - 1) & (chunk >= chunks - around)
+
+    def around_rows(chunk):
+        return pl.ds(pl.multiple_of((chunk - (chunks - around)) * piece, piece), piece)
+
+    def around_copy(step, chunk):
+        return remote(
+            terms.at[spans - 1, other_head(step), rows_of(chunk), :],
+            via.at[step, around_rows(chunk), :],
+            around_sends.at[step, chunk],
+            around_recvs.at[step, chunk],
+            {"segment": last_segment - 1},
+        )
+
+    def around_arrival(step, chunk):
+        return remote(
+            via.at[step, around_rows(chunk), :],
+            via.at[step, around_rows(chunk), :],
+            around_sends.at[step, chunk],
+            around_recvs.at[step, chunk],
+            {"segment": last_segment},
+        )
+
+    def around_onward(step, chunk):
+        return remote(
+            via.at[step, around_rows(chunk), :],
+            slots.at[spans - 1, me, rows_of(chunk), :],
+            around_sends.at[step, chunk],
+            term_recvs.at[spans - 1, me, chunk],
+            {"segment": last_segment, "head": other_head(step)},
+        )
+
+    def send_terms(span):
+        def send(index, carry):
+            chunk = chunks - 1 - index
+
+            @pl.when(detours(span, chunk))
+            def _():
+                for step in range(1, heads):
+                    around_copy(step, chunk).start()
+
             return carry
 
-        lax.fori_loop(0, heads, term, 0)
-        for chunk in range(chunks):
-            for step in range(1, heads):
-                term_copy(span, step, chunk).start()
+        if around:
+            lax.fori_loop(0, around, send, 0)
+
+        def send_straight(chunk, carry):
+            @pl.when(jnp.logical_not(detours(span, chunk)))
+            def _():
+                for step in range(1, heads):
+                    term_copy(span, step, chunk).start()
+
+            return carry
+
+        lax.fori_loop(0, chunks, send_straight, 0)
 
     @pl.when(segment == 0)
     def _():
@@ -416,8 +509,17 @@
 
     @pl.when(segment > 0)
     def _():
-        for chunk in range(chunks):
+        each_spread(0, wait_send)
+        for span in range(1, spans):
+            pl.semaphore_wait(ready, heads - 1)
+            each_spread(span, start)
+            each_spread(span, wait_send)
+
+        def one(chunk, carry):
             relay(0, chunk)
+            return carry
+
+        lax.fori_loop(0, chunks, one, 0)
 
     for part in (1, 2, 0):
         loads[part].wait()
@@ -426,46 +528,94 @@
     def block(span, carry):
         project(span)
 
+        @pl.when((segment == 0) & (span + 1 < spans))
+        def _():
+            each_spread(span + 1, start)
+
+            for away in range(1, segments):
+                for step in range(1, heads):
+                    signal(ready, {"segment": away, "head": other_head(step)})
+
         def gradient_step(step, inner):
             gradients(span, step)
+
+            @pl.when(step == 0)
+            def _():
+                between(span, 0, unit)
+
             return inner
 
         lax.fori_loop(0, chips, gradient_step, 0)
-        between(span, 0)
-
-        def orthogonal_step(index, inner):
-            orthogonalize(span, index)
-
-            @pl.when(index + 1 < chunks)
-            def _():
-                between(span, index + 1)
-
-            return inner
-
-        lax.fori_loop(0, 3, orthogonal_step, 0)
+        between(span, unit, 2 * unit)
+        orthogonalize(span)
+        between(span, 5 * unit, unit)
         update()
         read_out(span)
+        between(span, 6 * unit, 2 * unit)
+        send_terms(span)
         return carry
 
     lax.fori_loop(0, spans, block, 0)
-    for chunk in range(chunks):
+
+    def last(chunk, carry):
         finish(spans - 1, chunk)
-
-    each_spread(lambda copy: copy.wait_send())
+        return carry
+
+    lax.fori_loop(0, chunks, last, 0)
+
+    if around:
+
+        @pl.when(segment == last_segment - 1)
+        def _():
+            def pass_on(index, carry):
+                for step in range(1, heads):
+                    around_arrival(step, chunks - 1 - index).wait_recv()
+                    around_onward(step, chunks - 1 - index).start()
+                return carry
+
+            lax.fori_loop(0, around, pass_on, 0)
+
+            def settle(index, carry):
+                for step in range(1, heads):
+                    around_onward(step, chunks - 1 - index).wait_send()
+                return carry
+
+            lax.fori_loop(0, around, settle, 0)
+
+    @pl.when(segment == 0)
+    def _():
+        for span in range(spans):
+            each_spread(span, wait_send)
 
     def drain(span, carry):
-        for chunk in range(chunks):
-            for step in range(1, heads):
-                term_copy(span, step, chunk).wait_send()
-
-            @pl.when(segment > 0)
+        def drain_chunk(chunk, inner):
+            @pl.when(jnp.logical_not(detours(span, chunk)))
+            def _():
+                for step in range(1, heads):
+                    term_copy(span, step, chunk).wait_send()
+
+            @pl.when(detours(span, chunk))
+            def _():
+                for step in range(1, heads):
+                    around_copy(step, chunk).wait_send()
+
+            @pl.when((segment > 0) & (chunk < straight))
             def _():
                 for step in range(1, heads):
                     relay_copy(span, step, chunk).wait_send()
 
             @pl.when(segment < last_segment)
             def _():
-                hop(span, chunk).wait_send()
+                hop(span, 0, chunk).wait_send()
+
+                @pl.when(chunk >= straight)
+                def _():
+                    for step in range(1, heads):
+                        hop(span, step, chunk).wait_send()
+
+            return inner
+
+        lax.fori_loop(0, chunks, drain_chunk, 0)
 
         for part in range(2):
             for step in range(1, chips):
@@ -485,7 +635,7 @@
     features = w_qkv.shape[1]
     inner, wide = w_one.shape[2:]
     tokens = devices * rows
-    chunks = 4
+    chunks = 8
     vmem = pl.BlockSpec(memory_space=pltpu.VMEM)
     anywhere = pl.BlockSpec(memory_space=pl.ANY)
     low = jnp.bfloat16
@@ -524,9 +674,13 @@
             dma((spans, 2, devices // 2)),
             dma((spans, heads, chunks)),
             dma((spans, heads, chunks)),
-            dma((spans, chunks)),
             dma((spans, heads, chunks)),
-        ],
+            dma((spans, heads, chunks)),
+            dma((heads, chunks)),
+            dma((heads, chunks)),
+            pltpu.SemaphoreType.REGULAR,
+        ]
+        + ([pltpu.VMEM((heads, 4 * (chunks // 8) * (rows // chunks), width), low)] if segments > 1 else []),
         compiler_params=pltpu.CompilerParams(
             collective_id=0, has_side_effects=True, vmem_limit_bytes=67043328
         ),

time: 184 us -> 155 us (0.84)
  Pallas kernels: 182 us -> 153 us
    pallas_call x1, Pallas kernels: 182 us -> 153 us  [shards(): pl.pallas_call(functools.partial(step_kernel, segments, devices, heads, c...]
where the time goes in v2:
time: 155 us
  Pallas kernels  153 us (99%)
  local copies, waits for them, and re-layouts  1.87 us (1%)
    pallas_call x1, Pallas kernels, shards(): pl.pallas_call(functools.partial(step_kernel, segments, devices, heads, c...  153 us

profile of v2, /device:TPU:3, one launch (start us, length us, event | category | flops | bytes accessed | tf_op | source)
XLA Modules:
  0.0 155.0 jit_solution(2638435749037677426)
XLA Ops:
  0.0 153.1 %step.1 = bf16[2,128,1024]{2,1,0:T(8,128)(2,1)} custom-call(bf16[2,128,1024]{2,1,0:T(8,128)(2,1)} %stream_hbm.1, f32[1,4096]{1,0:T(1,128)} %in_gain_ref.1, bf16[3,4096,512]{2,1,0:T(8,128)(2,1)} %bitcast.11, f32[2,512]{1,0:T(2,128)} %bitcast.17, bf16[512,768]{1,0:T(8,128)(2,1)} %bitcast.14, bf16[512,768]{1,0:T(8,128)(2,1)} %bitcast.15, ...), custom_call_target="tpu_custom_call" | custom-call | tf_op jit(solution)/shard_map/step/pallas_call | solution.py:643
  153.1 1.9 %copy.12 = bf16[1,2,128,1024]{3,2,1,0:T(8,128)(2,1)} copy(bf16[1,2,128,1024]{3,2,1,0:T(8,128)(2,1)} %bitcast.13) | data formatting | bytes 1048576

commit v3 on v2

--- a/solution.py
+++ b/solution.py
@@ -70,6 +70,7 @@
     down_init,
     whole,
     scaled,
+    row_scale,
     sums,
     both,
     queries,
@@ -85,6 +86,8 @@
     own_sems,
     spread_sends,
     arrivals,
+    own_recvs,
+    pass_recvs,
     far_sends,
     far_recvs,
     near_sends,
@@ -92,10 +95,15 @@
     term_sends,
     term_recvs,
     hop_sends,
+    straight_sends,
     relay_sends,
     around_sends,
     around_recvs,
     ready,
+    pass_sends,
+    aside_sends,
+    aside_recvs,
+    aside,
     *vias,
 ):
     segment = lax.axis_index("segment")
@@ -108,10 +116,9 @@
     partner = {"seq": 2 * chip + 1 - core}
     piece = rows // chunks
     unit = chunks // 8
-    around = 4 * unit if segments > 1 else 0
+    around = 3 * unit if segments > 1 else 0
     via = vias[0] if around else None
     last_segment = segments - 1
-    straight = chunks - 1
 
     loads = [pltpu.make_async_copy(qkv_hbm.at[part], qkv.at[part], qkv_sems.at[part]) for part in range(3)]
     fast_loads = [
@@ -124,13 +131,19 @@
         copy.start()
 
     def other_head(step):
-        return lax.rem(me + step, heads)
+        up, down = step - 1, heads - step
+        upward = jnp.where(up >= me, up + 1, up)
+        downward = jnp.where(down > me, down, down - 1)
+        return jnp.where(2 * me < heads, downward, upward)
 
     barrier = pltpu.get_barrier_semaphore()
     for away in range(segments):
         for step in range(heads):
             if away or step:
-                signal(barrier, {"segment": lax.rem(segment + away, segments), "head": other_head(step)})
+                signal(
+                    barrier,
+                    {"segment": lax.rem(segment + away, segments), "head": lax.rem(me + step, heads)},
+                )
     for step in range(1, chips):
         signal(barrier, {"seq": 2 * lax.rem(chip + step, chips) + core})
     signal(barrier, partner)
@@ -147,32 +160,38 @@
     def place(span, origin, chunk):
         return whole.at[span, rows_of(chunk), columns_of(origin)]
 
+    def await_arrival(like, semaphore):
+        remote(like, like, semaphore, semaphore, partner).wait_recv()
+
+    def await_sent(like, semaphore):
+        remote(like, like, semaphore, semaphore, partner).wait_send()
+
+    def as_many(blocks, count):
+        return terms.at[0, pl.ds(0, blocks), pl.ds(0, count * piece), :]
+
     def spread(span, step, chunk):
         return remote(
             stream_hbm.at[span, rows_of(chunk), :],
             place(span, me, chunk),
-            spread_sends.at[span, step, chunk],
-            arrivals.at[span, me, chunk],
+            spread_sends.at[span],
+            arrivals.at[span, me],
             {"segment": 0, "head": other_head(step)},
         )
 
-    def each_spread(span, action):
-        share = chunks // segments
-
+    share = chunks // segments
+
+    def start_spread(span):
         def one(index, carry):
             for step in range(1, heads):
-                action(spread(span, step, segment * share + index))
+                spread(span, step, segment * share + index).start()
             return carry
 
         lax.fori_loop(0, share, one, 0)
 
-    def start(copy):
-        copy.start()
-
-    def wait_send(copy):
-        copy.wait_send()
-
-    each_spread(0, start)
+    def settle_spread(span):
+        await_sent(as_many(heads - 1, share), spread_sends.at[span])
+
+    start_spread(0)
     for part in (1, 2, 0):
         loads[part].start()
     out_load.start()
@@ -200,28 +219,74 @@
     state[2] = down
     down_norm[...] = jnp.sqrt(jnp.sum(down * down, axis=1, keepdims=True))
 
-    def arrival(span, origin, chunk):
-        return remote(
-            place(span, origin, chunk),
-            place(span, origin, chunk),
-            hop_sends.at[span, 0, chunk],
-            arrivals.at[span, origin, chunk],
-            {"head": other_head(1)},
-        )
+    def goes_straight(span, chunk):
+        return (span > 0) & (chunk >= chunks - 2 * unit)
 
     def relay_copy(span, step, chunk):
         return remote(
             place(span, me, chunk),
             place(span, me, chunk),
-            relay_sends.at[span, step, chunk],
-            arrivals.at[span, me, chunk],
+            relay_sends.at[span],
+            arrivals.at[span, me],
             {"head": other_head(step)},
         )
 
+    def passing(side, origin, chunk):
+        return remote(
+            place(0, origin, chunk),
+            place(0, origin, chunk),
+            pass_sends.at[side, origin],
+            pass_recvs.at[origin, chunk],
+            {"head": me + 1 - 2 * side},
+        )
+
+    has_next = (me + 1 < heads, me >= 1)
+    passed_on = chunks - unit
+
+    def each_passing(side, distance, chunk, action):
+        origin = me - distance * (1 - 2 * side)
+
+        @pl.when(
+            (chunk >= 0) & (chunk < passed_on) & (origin >= 0) & (origin < heads) & has_next[side]
+        )
+        def _():
+            action(side, origin, chunk)
+
+    def pass_first_block():
+        def forward(side, origin, chunk):
+            await_arrival(place(0, origin, chunk), pass_recvs.at[origin, chunk])
+            passing(side, origin, chunk).start()
+
+        def moment(now, carry):
+            @pl.when(now < passed_on)
+            def _():
+                await_arrival(place(0, me, now), own_recvs.at[0, now])
+
+            @pl.when((now >= passed_on) & (now < chunks))
+            def _():
+                relay(0, now)
+
+            for side in range(2):
+                each_passing(side, 0, now, lambda *which: passing(*which).start())
+            for distance in range(1, heads - 1):
+                for side in range(2):
+                    each_passing(side, distance, now - distance, forward)
+            return carry
+
+        lax.fori_loop(0, chunks + heads - 2, moment, 0)
+
+    def settle_first_block():
+        def settle_passing(side, origin, chunk):
+            await_sent(as_many(1, passed_on), pass_sends.at[side, origin])
+
+        for distance in range(heads - 1):
+            for side in range(2):
+                each_passing(side, distance, 0, settle_passing)
+
     def relay(span, chunk):
-        arrival(span, me, chunk).wait_recv()
-
-        @pl.when(chunk < straight)
+        await_arrival(place(span, me, chunk), own_recvs.at[span, chunk])
+
+        @pl.when(jnp.logical_not(goes_straight(span, chunk)))
         def _():
             for step in range(1, heads):
                 relay_copy(span, step, chunk).start()
@@ -231,15 +296,26 @@
         sums[1] = jnp.zeros(sums.shape[1:], jnp.float32)
 
         def block(step, squares):
-            origin = other_head(step)
-
-            @pl.when(step > 0)
+            origin = lax.rem(me + step, heads)
+
+            first = (segment > 0) & (span == 0)
+            passed = jnp.where(origin < me, me + 1 < heads, me >= 1)
+
+            @pl.when((step > 0) & jnp.logical_not(first))
+            def _():
+                await_arrival(whole.at[span, :, columns_of(origin)], arrivals.at[span, origin])
+
+            @pl.when((step > 0) & first)
+            def _():
+                await_arrival(place(span, origin, passed_on), arrivals.at[span, origin])
+
+            @pl.when((step > 0) & first & jnp.logical_not(passed))
             def _():
                 def wait(chunk, carry):
-                    arrival(span, origin, chunk).wait_recv()
+                    await_arrival(place(span, origin, chunk), pass_recvs.at[origin, chunk])
                     return carry
 
-                lax.fori_loop(0, chunks, wait, 0)
+                lax.fori_loop(0, passed_on, wait, 0)
 
             here = columns_of(origin)
             values = whole[span, :, here].astype(jnp.float32)
@@ -249,7 +325,7 @@
             return squares + jnp.sum(values * values, axis=1, keepdims=True)
 
         squares = lax.fori_loop(0, heads, block, jnp.zeros((rows, 1), jnp.float32))
-        return lax.rsqrt(squares * (1.0 / features) + norm_eps)
+        row_scale[...] = lax.rsqrt(squares * (1.0 / features) + norm_eps)
 
     def rows_at(origin, count=1):
         return pl.ds(pl.multiple_of(origin * rows, rows), count * rows)
@@ -258,7 +334,7 @@
         return remote(
             both.at[span, part, rows_at(place_seq), :],
             both.at[span, part, rows_at(place_seq), :],
-            far_sends.at[span, part, step],
+            far_sends.at[span],
             far_recvs.at[span, part, step],
             {"seq": 2 * lax.rem(chip + step, chips) + core},
         )
@@ -268,13 +344,14 @@
         return remote(
             both.at[span, part, rows_at(origin), :],
             both.at[span, part, rows_at(origin), :],
-            near_sends.at[span, part, step],
-            near_recvs.at[span, part, step],
+            near_sends.at[span],
+            near_recvs.at[span, step],
             partner,
         )
 
-    def project(span):
-        scale = project_keys(span)
+    def project_pair(span):
+        project_keys(span)
+        scale = row_scale[...]
         own = rows_at(place_seq)
         both[span, 0, own, :] = (rms_scale(sums[0] * scale) * qk_gain_ref[1:2, :]).astype(jnp.bfloat16)
         diagonal = lax.broadcasted_iota(jnp.int32, (rows, rows), 0) == lax.broadcasted_iota(
@@ -289,17 +366,18 @@
                 far_copy(span, part, step).start()
         for part in range(2):
             near_copy(span, part, 0).start()
-        sums[0] = dot(scaled[...], qkv[0])
-        queries[...] = (rms_scale(sums[0] * scale) * qk_gain_ref[0:1, :]).astype(jnp.bfloat16)
+
+    def project_queries():
+        queries[...] = (rms_scale(dot(scaled[...], qkv[0]) * row_scale[...]) * qk_gain_ref[0:1, :]).astype(jnp.bfloat16)
 
     def finish(span, chunk):
         here = rows_of(chunk)
         total = whole[span, here, columns_of(me)].astype(jnp.float32) + terms[
             span, me, here, :
         ].astype(jnp.float32)
+        await_arrival(as_many(heads - 1, 1), term_recvs.at[span, chunk])
         for step in range(1, heads):
             origin = other_head(step)
-            term_arrival(span, origin, chunk).wait_recv()
             total += slots[span, origin, here, :].astype(jnp.float32)
         result_ref[span, here, :] = total.astype(jnp.bfloat16)
 
@@ -307,7 +385,7 @@
         def _():
             hop(span, 0, chunk).start()
 
-            @pl.when(chunk >= straight)
+            @pl.when(goes_straight(span, chunk))
             def _():
                 for step in range(1, heads):
                     hop(span, step, chunk).start()
@@ -317,31 +395,22 @@
         return remote(
             terms.at[span, target, rows_of(chunk), :],
             slots.at[span, me, rows_of(chunk), :],
-            term_sends.at[span, step, chunk],
-            term_recvs.at[span, me, chunk],
+            term_sends.at[span],
+            term_recvs.at[span, chunk],
             {"head": target},
-        )
-
-    def term_arrival(span, origin, chunk):
-        return remote(
-            slots.at[span, origin, rows_of(chunk), :],
-            slots.at[span, origin, rows_of(chunk), :],
-            hop_sends.at[span, 0, chunk],
-            term_recvs.at[span, origin, chunk],
-            {"head": other_head(1)},
         )
 
     def hop(span, step, chunk):
         return remote(
             result_ref.at[span, rows_of(chunk), :],
             place(span, me, chunk),
-            hop_sends.at[span, step, chunk],
-            arrivals.at[span, me, chunk],
-            {"segment": segment + 1, "head": other_head(step)},
-        )
-
-    def between(span, first, count):
-        @pl.when(span > 0)
+            straight_sends.at[span] if step else hop_sends.at[span],
+            arrivals.at[span, me] if step else own_recvs.at[span, chunk],
+            {"segment": segment + 1, "head": other_head(step) if step else me},
+        )
+
+    def finish_some(span, first, count):
+        @pl.when((segment < last_segment) & (span > 0))
         def _():
             def one(index, carry):
                 finish(span - 1, first + index)
@@ -349,6 +418,7 @@
 
             lax.fori_loop(0, count, one, 0)
 
+    def relay_some(span, first, count):
         @pl.when((segment > 0) & (span + 1 < spans))
         def _():
             def one(index, carry):
@@ -362,25 +432,14 @@
 
             @pl.when(step > 0)
             def _():
-                remote(
-                    both.at[span, part, rows_at(2 * lax.rem(chip + chips - step, chips) + core), :],
-                    both.at[span, part, rows_at(2 * lax.rem(chip + chips - step, chips) + core), :],
-                    far_sends.at[span, part, step],
-                    far_recvs.at[span, part, step],
-                    partner,
-                ).wait_recv()
+                there = rows_at(2 * lax.rem(chip + chips - step, chips) + core)
+                await_arrival(both.at[span, part, there, :], far_recvs.at[span, part, step])
                 near_copy(span, part, step).start()
 
         origin = lax.rem(chip + chips - step, chips)
-        for part in range(2):
-            twin = rows_at(2 * origin + 1 - core)
-            remote(
-                both.at[span, part, twin, :],
-                both.at[span, part, twin, :],
-                near_sends.at[span, part, step],
-                near_recvs.at[span, part, step],
-                partner,
-            ).wait_recv()
+        await_arrival(
+            both.at[span, :, rows_at(2 * origin + 1 - core), :], near_recvs.at[span, step]
+        )
         here = rows_at(2 * origin, 2)
         keys = both[span, 0, here, :]
         grads = both[span, 1, here, :]
@@ -405,7 +464,8 @@
             work[index] = (raw[index] * scales[index]).astype(jnp.bfloat16)
 
         def sweep(step, inner):
-            between(span, (3 + step) * unit, unit)
+            finish_some(span, (2 + step) * unit, (1 + step) * unit)
+            relay_some(span, (3 + step) * unit, (1 + step) * unit)
             current = [work[index] for index in range(3)]
             grams = [contract(matrix, matrix, (1, 1)).astype(jnp.bfloat16) for matrix in current]
             squares = [dot(gram, gram) for gram in grams]
@@ -446,35 +506,75 @@
                 normed_out, out_weights[:, origin * width : (origin + 1) * width]
             ).astype(jnp.bfloat16)
     def detours(span, chunk):
-        return (segment == last_segment) & (span == spans - 1) & (chunk >= chunks - around)
+        return (segment == last_segment) & (chunk >= chunks - around)
+
+    def steps_aside(span, chunk):
+        if segments == 1:
+            return segment < 0
+        return (segment == 0) & (span == 0) & ((chunk // unit == 2) | (chunk // unit == 4))
+
+    def aside_chunk(place_at):
+        return (2 + 2 * (place_at // unit)) * unit + lax.rem(place_at, unit)
+
+    def aside_rows(place_at):
+        return pl.ds(pl.multiple_of(place_at * piece, piece), piece)
+
+    def aside_copy(step, place_at):
+        return remote(
+            terms.at[0, other_head(step), rows_of(aside_chunk(place_at)), :],
+            aside.at[step, aside_rows(place_at), :],
+            aside_sends.at[0],
+            aside_recvs.at[place_at],
+            {"segment": 1},
+        )
+
+    def aside_onward(step, place_at):
+        return remote(
+            aside.at[step, aside_rows(place_at), :],
+            slots.at[0, me, rows_of(aside_chunk(place_at)), :],
+            aside_sends.at[0],
+            term_recvs.at[0, aside_chunk(place_at)],
+            {"segment": 0, "head": other_head(step)},
+        )
+
+    def each_aside(action):
+        def one(place_at, carry):
+            for step in range(1, heads):
+                action(step, place_at).start()
+            return carry
+
+        lax.fori_loop(0, 2 * unit, one, 0)
+
+    def pass_aside():
+        def one(place_at, carry):
+            await_arrival(as_many(heads - 1, 1), aside_recvs.at[place_at])
+            for step in range(1, heads):
+                aside_onward(step, place_at).start()
+            return carry
+
+        lax.fori_loop(0, 2 * unit, one, 0)
+
+    def settle_aside():
+        await_sent(as_many(heads - 1, 2 * unit), aside_sends.at[0])
 
     def around_rows(chunk):
         return pl.ds(pl.multiple_of((chunk - (chunks - around)) * piece, piece), piece)
 
-    def around_copy(step, chunk):
-        return remote(
-            terms.at[spans - 1, other_head(step), rows_of(chunk), :],
-            via.at[step, around_rows(chunk), :],
-            around_sends.at[step, chunk],
-            around_recvs.at[step, chunk],
+    def around_copy(span, step, chunk):
+        return remote(
+            terms.at[span, other_head(step), rows_of(chunk), :],
+            via.at[span, step, around_rows(chunk), :],
+            around_sends.at[span],
+            around_recvs.at[span, chunk - (chunks - around)],
             {"segment": last_segment - 1},
         )
 
-    def around_arrival(step, chunk):
-        return remote(
-            via.at[step, around_rows(chunk), :],
-            via.at[step, around_rows(chunk), :],
-            around_sends.at[step, chunk],
-            around_recvs.at[step, chunk],
-            {"segment": last_segment},
-        )
-
-    def around_onward(step, chunk):
-        return remote(
-            via.at[step, around_rows(chunk), :],
-            slots.at[spans - 1, me, rows_of(chunk), :],
-            around_sends.at[step, chunk],
-            term_recvs.at[spans - 1, me, chunk],
+    def around_onward(span, step, chunk):
+        return remote(
+            via.at[span, step, around_rows(chunk), :],
+            slots.at[span, me, rows_of(chunk), :],
+            around_sends.at[span],
+            term_recvs.at[span, chunk],
             {"segment": last_segment, "head": other_head(step)},
         )
 
@@ -485,15 +585,19 @@
             @pl.when(detours(span, chunk))
             def _():
                 for step in range(1, heads):
-                    around_copy(step, chunk).start()
+                    around_copy(span, step, chunk).start()
 
             return carry
 
         if around:
             lax.fori_loop(0, around, send, 0)
 
+            @pl.when((segment == 0) & (span == 0))
+            def _():
+                each_aside(aside_copy)
+
         def send_straight(chunk, carry):
-            @pl.when(jnp.logical_not(detours(span, chunk)))
+            @pl.when(jnp.logical_not(detours(span, chunk) | steps_aside(span, chunk)))
             def _():
                 for step in range(1, heads):
                     term_copy(span, step, chunk).start()
@@ -509,122 +613,150 @@
 
     @pl.when(segment > 0)
     def _():
-        each_spread(0, wait_send)
+        settle_spread(0)
         for span in range(1, spans):
             pl.semaphore_wait(ready, heads - 1)
-            each_spread(span, start)
-            each_spread(span, wait_send)
-
-        def one(chunk, carry):
-            relay(0, chunk)
-            return carry
-
-        lax.fori_loop(0, chunks, one, 0)
+            start_spread(span)
+            settle_spread(span)
+
+        @pl.when(segment == 1)
+        def _():
+            pass_aside()
+
+        pass_first_block()
 
     for part in (1, 2, 0):
         loads[part].wait()
     out_load.wait()
 
     def block(span, carry):
-        project(span)
+        @pl.when((segment > 0) | (span == 0))
+        def _():
+            project_pair(span)
+
+        @pl.when((segment == last_segment) & (span > 0))
+        def _():
+            send_terms(span - 1)
 
         @pl.when((segment == 0) & (span + 1 < spans))
         def _():
-            each_spread(span + 1, start)
+            start_spread(span + 1)
 
             for away in range(1, segments):
                 for step in range(1, heads):
                     signal(ready, {"segment": away, "head": other_head(step)})
 
+        relay_some(span, 0, unit)
+        project_queries()
+
         def gradient_step(step, inner):
             gradients(span, step)
 
             @pl.when(step == 0)
             def _():
-                between(span, 0, unit)
+                finish_some(span, 0, unit)
+                relay_some(span, unit, unit)
 
             return inner
 
         lax.fori_loop(0, chips, gradient_step, 0)
-        between(span, unit, 2 * unit)
+        finish_some(span, unit, unit)
+        relay_some(span, 2 * unit, unit)
         orthogonalize(span)
-        between(span, 5 * unit, unit)
+        finish_some(span, 5 * unit, 2 * unit)
+
+        @pl.when((segment == 0) & (span + 1 < spans))
+        def _():
+            project_pair(span + 1)
+
         update()
         read_out(span)
-        between(span, 6 * unit, 2 * unit)
-        send_terms(span)
+        finish_some(span, 7 * unit, unit)
+        relay_some(span, 6 * unit, 2 * unit)
+
+        @pl.when((segment < last_segment) | (span == spans - 1))
+        def _():
+            send_terms(span)
+
         return carry
 
     lax.fori_loop(0, spans, block, 0)
-
-    def last(chunk, carry):
-        finish(spans - 1, chunk)
-        return carry
-
-    lax.fori_loop(0, chunks, last, 0)
-
-    if around:
-
-        @pl.when(segment == last_segment - 1)
-        def _():
-            def pass_on(index, carry):
-                for step in range(1, heads):
-                    around_arrival(step, chunks - 1 - index).wait_recv()
-                    around_onward(step, chunks - 1 - index).start()
-                return carry
-
-            lax.fori_loop(0, around, pass_on, 0)
-
-            def settle(index, carry):
-                for step in range(1, heads):
-                    around_onward(step, chunks - 1 - index).wait_send()
-                return carry
-
-            lax.fori_loop(0, around, settle, 0)
 
     @pl.when(segment == 0)
     def _():
         for span in range(spans):
-            each_spread(span, wait_send)
-
-    def drain(span, carry):
-        def drain_chunk(chunk, inner):
-            @pl.when(jnp.logical_not(detours(span, chunk)))
-            def _():
+            settle_spread(span)
+        if segments > 1:
+            settle_aside()
+
+    @pl.when(segment > 0)
+    def _():
+        settle_first_block()
+        await_sent(as_many(heads - 1, unit), relay_sends.at[0])
+        for span in range(1, spans):
+            await_sent(as_many(heads - 1, chunks - 2 * unit), relay_sends.at[span])
+
+        @pl.when(segment == 1)
+        def _():
+            settle_aside()
+
+    def settle_terms(span):
+        beside = 2 * unit if segments > 1 and span == 0 else 0
+
+        @pl.when((segment > 0) & (segment < last_segment))
+        def _():
+            await_sent(as_many(heads - 1, chunks), term_sends.at[span])
+
+        @pl.when((segment == 0) & (segment < last_segment))
+        def _():
+            await_sent(as_many(heads - 1, chunks - beside), term_sends.at[span])
+
+        @pl.when(segment == last_segment)
+        def _():
+            await_sent(as_many(heads - 1, chunks - around), term_sends.at[span])
+            if around:
+                await_sent(as_many(heads - 1, around), around_sends.at[span])
+
+    def settle_hops(span):
+        @pl.when(segment < last_segment)
+        def _():
+            await_sent(as_many(1, chunks), hop_sends.at[span])
+            if span:
+                await_sent(as_many(heads - 1, 2 * unit), straight_sends.at[span])
+
+    for span in range(spans):
+        if span + 1 < spans:
+            settle_terms(span)
+            settle_hops(span)
+        if chips > 1:
+            await_sent(both.at[span, :, pl.ds(0, (chips - 1) * rows), :], far_sends.at[span])
+        await_sent(both.at[span, :, pl.ds(0, chips * rows), :], near_sends.at[span])
+
+    def last(index, carry):
+        finish(index // chunks, lax.rem(index, chunks))
+        return carry
+
+    lax.fori_loop(jnp.where(segment < last_segment, (spans - 1) * chunks, 0), spans * chunks, last, 0)
+
+    if around:
+
+        @pl.when(segment == last_segment - 1)
+        def _():
+            def pass_on(index, carry):
+                span, chunk = index // around, chunks - 1 - lax.rem(index, around)
+                await_arrival(
+                    as_many(heads - 1, 1), around_recvs.at[span, chunk - (chunks - around)]
+                )
                 for step in range(1, heads):
-                    term_copy(span, step, chunk).wait_send()
-
-            @pl.when(detours(span, chunk))
-            def _():
-                for step in range(1, heads):
-                    around_copy(step, chunk).wait_send()
-
-            @pl.when((segment > 0) & (chunk < straight))
-            def _():
-                for step in range(1, heads):
-                    relay_copy(span, step, chunk).wait_send()
-
-            @pl.when(segment < last_segment)
-            def _():
-                hop(span, 0, chunk).wait_send()
-
-                @pl.when(chunk >= straight)
-                def _():
-                    for step in range(1, heads):
-                        hop(span, step, chunk).wait_send()
-
-            return inner
-
-        lax.fori_loop(0, chunks, drain_chunk, 0)
-
-        for part in range(2):
-            for step in range(1, chips):
-                far_copy(span, part, step).wait_send()
-            for step in range(chips):
-                near_copy(span, part, step).wait_send()
-        return carry
-
-    lax.fori_loop(0, spans, drain, 0)
+                    around_onward(span, step, chunk).start()
+                return carry
+
+            lax.fori_loop(0, spans * around, pass_on, 0)
+            for span in range(spans):
+                await_sent(as_many(heads - 1, around), around_sends.at[span])
+
+    settle_terms(spans - 1)
+    settle_hops(spans - 1)
 
 
 def shards(stream, in_gain, w_qkv, qk_gain, w_one, w_three, w_two, token_rate, out_gain, w_out):
@@ -653,6 +785,7 @@
             pltpu.VMEM((wide, inner), low),
             pltpu.VMEM((spans, rows, features), low),
             pltpu.VMEM((rows, features), low),
+            pltpu.VMEM((rows, 1), jnp.float32),
             pltpu.VMEM((2, rows, inner), jnp.float32),
             pltpu.VMEM((spans, 2, tokens, inner), low),
             pltpu.VMEM((rows, inner), low),
@@ -666,21 +799,28 @@
             dma((3,)),
             dma((4,)),
             dma((spans,)),
-            dma((spans, heads, chunks)),
-            dma((spans, heads, chunks)),
+            dma((spans,)),
+            dma((spans, heads)),
+            dma((spans, chunks)),
+            dma((heads, chunks)),
+            dma((spans,)),
             dma((spans, 2, devices // 2)),
-            dma((spans, 2, devices // 2)),
-            dma((spans, 2, devices // 2)),
-            dma((spans, 2, devices // 2)),
-            dma((spans, heads, chunks)),
-            dma((spans, heads, chunks)),
-            dma((spans, heads, chunks)),
-            dma((spans, heads, chunks)),
-            dma((heads, chunks)),
-            dma((heads, chunks)),
+            dma((spans,)),
+            dma((spans, devices // 2)),
+            dma((spans,)),
+            dma((spans, chunks)),
+            dma((spans,)),
+            dma((spans,)),
+            dma((spans,)),
+            dma((spans,)),
+            dma((spans, 3 * (chunks // 8))),
             pltpu.SemaphoreType.REGULAR,
+            dma((2, heads)),
+            dma((1,)),
+            dma((chunks // 4,)),
+            pltpu.VMEM((heads, rows // 4, width), low),
         ]
-        + ([pltpu.VMEM((heads, 4 * (chunks // 8) * (rows // chunks), width), low)] if segments > 1 else []),
+        + ([pltpu.VMEM((spans, heads, 3 * (chunks // 8) * (rows // chunks), width), low)] if segments > 1 else []),
         compiler_params=pltpu.CompilerParams(
             collective_id=0, has_side_effects=True, vmem_limit_bytes=67043328
         ),

time: 155 us -> 142 us (0.916)
  Pallas kernels: 153 us -> 140 us
    pallas_call x1, Pallas kernels: 153 us -> 140 us  [shards(): pl.pallas_call(functools.partial(step_kernel, segments, devices, heads, c...]
where the time goes in v3:
time: 142 us
  Pallas kernels  140 us (99%)
  local copies, waits for them, and re-layouts  1.87 us (1%)
    pallas_call x1, Pallas kernels, shards(): pl.pallas_call(functools.partial(step_kernel, segments, devices, heads, c...  140 us

profile of v3, /device:TPU:3, one launch (start us, length us, event | category | flops | bytes accessed | tf_op | source)
XLA Modules:
  0.0 141.7 jit_solution(2017322334178559354)
XLA Ops:
  0.0 139.8 %step.1 = bf16[2,128,1024]{2,1,0:T(8,128)(2,1)} custom-call(bf16[2,128,1024]{2,1,0:T(8,128)(2,1)} %stream_hbm.1, f32[1,4096]{1,0:T(1,128)} %in_gain_ref.1, bf16[3,4096,512]{2,1,0:T(8,128)(2,1)} %bitcast.11, f32[2,512]{1,0:T(2,128)} %bitcast.17, bf16[512,768]{1,0:T(8,128)(2,1)} %bitcast.14, bf16[512,768]{1,0:T(8,128)(2,1)} %bitcast.15, ...), custom_call_target="tpu_custom_call" | custom-call | tf_op jit(solution)/shard_map/step/pallas_call | solution.py:775
  139.8 1.9 %copy.12 = bf16[1,2,128,1024]{3,2,1,0:T(8,128)(2,1)} copy(bf16[1,2,128,1024]{3,2,1,0:T(8,128)(2,1)} %bitcast.13) | data formatting | bytes 1048576

commit v4 on v3

--- a/solution.py
+++ b/solution.py
@@ -220,7 +220,7 @@
     down_norm[...] = jnp.sqrt(jnp.sum(down * down, axis=1, keepdims=True))
 
     def goes_straight(span, chunk):
-        return (span > 0) & (chunk >= chunks - 2 * unit)
+        return chunk >= chunks - jnp.where(span > 0, 2 * unit, unit)
 
     def relay_copy(span, step, chunk):
         return remote(
@@ -241,7 +241,7 @@
         )
 
     has_next = (me + 1 < heads, me >= 1)
-    passed_on = chunks - unit
+    passed_on = chunks - 5 * unit
 
     def each_passing(side, distance, chunk, action):
         origin = me - distance * (1 - 2 * side)
@@ -258,19 +258,20 @@
             passing(side, origin, chunk).start()
 
         def moment(now, carry):
-            @pl.when(now < passed_on)
-            def _():
-                await_arrival(place(0, me, now), own_recvs.at[0, now])
-
-            @pl.when((now >= passed_on) & (now < chunks))
-            def _():
-                relay(0, now)
-
-            for side in range(2):
-                each_passing(side, 0, now, lambda *which: passing(*which).start())
             for distance in range(1, heads - 1):
                 for side in range(2):
                     each_passing(side, distance, now - distance, forward)
+
+            @pl.when(now < passed_on)
+            def _():
+                await_arrival(place(0, me, now), own_recvs.at[0, now])
+
+            @pl.when((now >= passed_on) & (now < chunks))
+            def _():
+                relay(0, now)
+
+            for side in range(2):
+                each_passing(side, 0, now, lambda *which: passing(*which).start())
             return carry
 
         lax.fori_loop(0, chunks + heads - 2, moment, 0)
@@ -307,7 +308,10 @@
 
             @pl.when((step > 0) & first)
             def _():
-                await_arrival(place(span, origin, passed_on), arrivals.at[span, origin])
+                direct = pl.ds(passed_on * piece, (chunks - passed_on) * piece)
+                await_arrival(
+                    whole.at[span, direct, columns_of(origin)], arrivals.at[span, origin]
+                )
 
             @pl.when((step > 0) & first & jnp.logical_not(passed))
             def _():
@@ -454,6 +458,16 @@
         rights[1, here, :] = (backward * gated).astype(jnp.bfloat16)
         rights[2, here, :] = (gated * pre_up).astype(jnp.bfloat16)
 
+    def symmetric(upper, last_block):
+        return jnp.concatenate(
+            [upper, jnp.concatenate([upper[:, half:].T, last_block], axis=1)], axis=0
+        )
+
+    def mixed(gram, square):
+        return (ns_second * gram.astype(jnp.float32) + ns_third * square).astype(jnp.bfloat16)
+
+    half = work.shape[1] // 2
+
     def orthogonalize(span):
         raw = [contract(both[span, index // 2], rights[index], (0, 0)) for index in range(3)]
         scales = [
@@ -464,14 +478,19 @@
             work[index] = (raw[index] * scales[index]).astype(jnp.bfloat16)
 
         def sweep(step, inner):
-            finish_some(span, (2 + step) * unit, (1 + step) * unit)
+            finish_some(span, (4 + step) * unit, unit)
             relay_some(span, (3 + step) * unit, (1 + step) * unit)
             current = [work[index] for index in range(3)]
-            grams = [contract(matrix, matrix, (1, 1)).astype(jnp.bfloat16) for matrix in current]
-            squares = [dot(gram, gram) for gram in grams]
+            grams = [
+                symmetric(
+                    contract(matrix[:half], matrix, (1, 1)).astype(jnp.bfloat16),
+                    contract(matrix[half:], matrix[half:], (1, 1)).astype(jnp.bfloat16),
+                )
+                for matrix in current
+            ]
             mixings = [
-                (ns_second * gram.astype(jnp.float32) + ns_third * square).astype(jnp.bfloat16)
-                for gram, square in zip(grams, squares)
+                symmetric(mixed(gram[:half], dot(gram[:half], gram)), mixed(gram[half:, half:], dot(gram[half:], gram[:, half:])))
+                for gram in grams
             ]
             for index in range(3):
                 work[index] = (
@@ -483,16 +502,33 @@
         lax.fori_loop(0, NS_STEPS, sweep, 0)
 
     def update():
-        for index, axis, target in (
-            (0, 0, wide_norms[0]),
-            (1, 0, wide_norms[1]),
-            (2, 1, down_norm[...]),
-        ):
-            moved = state[index] - update_step * work[index].astype(jnp.float32)
-            length = jnp.sqrt(jnp.sum(moved * moved, axis=axis, keepdims=True)) + norm_eps
-            fresh = moved * (target / length)
-            work[index] = fresh.astype(jnp.bfloat16)
-            state[index] = fresh
+        inner, wide = work.shape[1:]
+
+        def moved(index, here, there):
+            return state[index, here, there] - update_step * work[index, here, there].astype(
+                jnp.float32
+            )
+
+        def store(index, here, there, fresh):
+            work[index, here, there] = fresh.astype(jnp.bfloat16)
+            state[index, here, there] = fresh
+
+        for index in range(2):
+            for column in range(0, wide, 256):
+                there = slice(column, column + 256)
+                squares = jnp.zeros((1, 256), jnp.float32)
+                for row in range(0, inner, 64):
+                    part = moved(index, slice(row, row + 64), there)
+                    squares += jnp.sum(part * part, axis=0, keepdims=True)
+                factor = wide_norms[index, :, there] / (jnp.sqrt(squares) + norm_eps)
+                for row in range(0, inner, 64):
+                    here = slice(row, row + 64)
+                    store(index, here, there, moved(index, here, there) * factor)
+        for row in range(0, inner, 32):
+            here = slice(row, row + 32)
+            part = moved(2, here, slice(None))
+            length = jnp.sqrt(jnp.sum(part * part, axis=1, keepdims=True)) + norm_eps
+            store(2, here, slice(None), part * (down_norm[here, :] / length))
 
     def read_out(span):
         gate_out = dot(queries[...], work[0])
@@ -654,29 +690,28 @@
 
             @pl.when(step == 0)
             def _():
-                finish_some(span, 0, unit)
+                finish_some(span, 0, 2 * unit)
                 relay_some(span, unit, unit)
 
             return inner
 
         lax.fori_loop(0, chips, gradient_step, 0)
-        finish_some(span, unit, unit)
+        finish_some(span, 2 * unit, 2 * unit)
         relay_some(span, 2 * unit, unit)
         orthogonalize(span)
-        finish_some(span, 5 * unit, 2 * unit)
-
-        @pl.when((segment == 0) & (span + 1 < spans))
-        def _():
-            project_pair(span + 1)
+        finish_some(span, 6 * unit, 2 * unit)
 
         update()
         read_out(span)
-        finish_some(span, 7 * unit, unit)
         relay_some(span, 6 * unit, 2 * unit)
 
         @pl.when((segment < last_segment) | (span == spans - 1))
         def _():
             send_terms(span)
+
+        @pl.when((segment == 0) & (span + 1 < spans))
+        def _():
+            project_pair(span + 1)
 
         return carry
 
@@ -692,7 +727,7 @@
     @pl.when(segment > 0)
     def _():
         settle_first_block()
-        await_sent(as_many(heads - 1, unit), relay_sends.at[0])
+        await_sent(as_many(heads - 1, chunks - unit - passed_on), relay_sends.at[0])
         for span in range(1, spans):
             await_sent(as_many(heads - 1, chunks - 2 * unit), relay_sends.at[span])
 
@@ -721,8 +756,7 @@
         @pl.when(segment < last_segment)
         def _():
             await_sent(as_many(1, chunks), hop_sends.at[span])
-            if span:
-                await_sent(as_many(heads - 1, 2 * unit), straight_sends.at[span])
+            await_sent(as_many(heads - 1, 2 * unit if span else unit), straight_sends.at[span])
 
     for span in range(spans):
         if span + 1 < spans:

time: 142 us -> 135 us (0.951)
  Pallas kernels: 140 us -> 133 us
    pallas_call x1, Pallas kernels: 140 us -> 133 us  [shards(): pl.pallas_call(functools.partial(step_kernel, segments, devices, heads, c...]
where the time goes in v4:
time: 135 us
  Pallas kernels  133 us (99%)
  local copies, waits for them, and re-layouts  1.87 us (1%)
    pallas_call x1, Pallas kernels, shards(): pl.pallas_call(functools.partial(step_kernel, segments, devices, heads, c...  133 us

profile of v4, /device:TPU:3, one launch (start us, length us, event | category | flops | bytes accessed | tf_op | source)
XLA Modules:
  0.0 135.0 jit_solution(1451695558344830030)
XLA Ops:
  0.0 133.1 %step.1 = bf16[2,128,1024]{2,1,0:T(8,128)(2,1)} custom-call(bf16[2,128,1024]{2,1,0:T(8,128)(2,1)} %stream_hbm.1, f32[1,4096]{1,0:T(1,128)} %in_gain_ref.1, bf16[3,4096,512]{2,1,0:T(8,128)(2,1)} %bitcast.11, f32[2,512]{1,0:T(2,128)} %bitcast.17, bf16[512,768]{1,0:T(8,128)(2,1)} %bitcast.14, bf16[512,768]{1,0:T(8,128)(2,1)} %bitcast.15, ...), custom_call_target="tpu_custom_call" | custom-call | tf_op jit(solution)/shard_map/step/pallas_call | solution.py:809
  133.1 1.9 %copy.12 = bf16[1,2,128,1024]{3,2,1,0:T(8,128)(2,1)} copy(bf16[1,2,128,1024]{3,2,1,0:T(8,128)(2,1)} %bitcast.13) | data formatting | bytes 1048576

commit v5 on v4

--- a/solution.py
+++ b/solution.py
@@ -478,7 +478,7 @@
             work[index] = (raw[index] * scales[index]).astype(jnp.bfloat16)
 
         def sweep(step, inner):
-            finish_some(span, (4 + step) * unit, unit)
+            finish_some(span, (3 + step) * unit, unit)
             relay_some(span, (3 + step) * unit, (1 + step) * unit)
             current = [work[index] for index in range(3)]
             grams = [
@@ -690,16 +690,16 @@
 
             @pl.when(step == 0)
             def _():
-                finish_some(span, 0, 2 * unit)
+                finish_some(span, 0, unit)
                 relay_some(span, unit, unit)
 
             return inner
 
         lax.fori_loop(0, chips, gradient_step, 0)
-        finish_some(span, 2 * unit, 2 * unit)
+        finish_some(span, unit, 2 * unit)
         relay_some(span, 2 * unit, unit)
         orthogonalize(span)
-        finish_some(span, 6 * unit, 2 * unit)
+        finish_some(span, 5 * unit, 3 * unit)
 
         update()
         read_out(span)

time: 135 us -> 134 us (level)
  Pallas kernels: 133 us -> 131 us
    pallas_call x1, Pallas kernels: 133 us -> 131 us  [shards(): pl.pallas_call(functools.partial(step_kernel, segments, devices, heads, c...]
where the time goes in v5:
time: 134 us; the launch traced here: 133 us
  Pallas kernels  131 us (98%)
  local copies, waits for them, and re-layouts  1.87 us (1%)
    pallas_call x1, Pallas kernels, shards(): pl.pallas_call(functools.partial(step_kernel, segments, devices, heads, c...  131 us

profile of v5, /device:TPU:3, one launch (start us, length us, event | category | flops | bytes accessed | tf_op | source)
XLA Modules:
  0.0 133.2 jit_solution(17131414180507572520)
XLA Ops:
  0.0 131.3 %step.1 = bf16[2,128,1024]{2,1,0:T(8,128)(2,1)} custom-call(bf16[2,128,1024]{2,1,0:T(8,128)(2,1)} %stream_hbm.1, f32[1,4096]{1,0:T(1,128)} %in_gain_ref.1, bf16[3,4096,512]{2,1,0:T(8,128)(2,1)} %bitcast.11, f32[2,512]{1,0:T(2,128)} %bitcast.17, bf16[512,768]{1,0:T(8,128)(2,1)} %bitcast.14, bf16[512,768]{1,0:T(8,128)(2,1)} %bitcast.15, ...), custom_call_target="tpu_custom_call" | custom-call | tf_op jit(solution)/shard_map/step/pallas_call | solution.py:809
  131.4 1.9 %copy.12 = bf16[1,2,128,1024]{3,2,1,0:T(8,128)(2,1)} copy(bf16[1,2,128,1024]{3,2,1,0:T(8,128)(2,1)} %bitcast.13) | data formatting | bytes 1048576

commit v6 on v5

--- a/solution.py
+++ b/solution.py
@@ -297,7 +297,7 @@
         sums[1] = jnp.zeros(sums.shape[1:], jnp.float32)
 
         def block(step, squares):
-            origin = lax.rem(me + step, heads)
+            origin = jnp.where(step == 0, me, other_head(heads - step))
 
             first = (segment > 0) & (span == 0)
             passed = jnp.where(origin < me, me + 1 < heads, me >= 1)
@@ -478,7 +478,7 @@
             work[index] = (raw[index] * scales[index]).astype(jnp.bfloat16)
 
         def sweep(step, inner):
-            finish_some(span, (3 + step) * unit, unit)
+            finish_some(span, (3 + step) * unit, (1 + step) * unit)
             relay_some(span, (3 + step) * unit, (1 + step) * unit)
             current = [work[index] for index in range(3)]
             grams = [
@@ -699,7 +699,7 @@
         finish_some(span, unit, 2 * unit)
         relay_some(span, 2 * unit, unit)
         orthogonalize(span)
-        finish_some(span, 5 * unit, 3 * unit)
+        finish_some(span, 6 * unit, 2 * unit)
 
         update()
         read_out(span)

time: 134 us -> 133 us (level)
  no operation moved by 1% of the time
where the time goes in v6:
time: 133 us
  Pallas kernels  131 us (98%)
  local copies, waits for them, and re-layouts  1.87 us (1%)
    pallas_call x1, Pallas kernels, shards(): pl.pallas_call(functools.partial(step_kernel, segments, devices, heads, c...  131 us

profile of v6, /device:TPU:3, one launch (start us, length us, event | category | flops | bytes accessed | tf_op | source)
XLA Modules:
  0.0 133.3 jit_solution(4761836798910457116)
XLA Ops:
  0.0 131.4 %step.1 = bf16[2,128,1024]{2,1,0:T(8,128)(2,1)} custom-call(bf16[2,128,1024]{2,1,0:T(8,128)(2,1)} %stream_hbm.1, f32[1,4096]{1,0:T(1,128)} %in_gain_ref.1, bf16[3,4096,512]{2,1,0:T(8,128)(2,1)} %bitcast.11, f32[2,512]{1,0:T(2,128)} %bitcast.17, bf16[512,768]{1,0:T(8,128)(2,1)} %bitcast.14, bf16[512,768]{1,0:T(8,128)(2,1)} %bitcast.15, ...), custom_call_target="tpu_custom_call" | custom-call | tf_op jit(solution)/shard_map/step/pallas_call | solution.py:809
  131.4 1.9 %copy.12 = bf16[1,2,128,1024]{3,2,1,0:T(8,128)(2,1)} copy(bf16[1,2,128,1024]{3,2,1,0:T(8,128)(2,1)} %bitcast.13) | data formatting | bytes 1048576

commit v7 on v6

--- a/solution.py
+++ b/solution.py
@@ -358,6 +358,8 @@
         scale = row_scale[...]
         own = rows_at(place_seq)
         both[span, 0, own, :] = (rms_scale(sums[0] * scale) * qk_gain_ref[1:2, :]).astype(jnp.bfloat16)
+        for step in range(1, chips):
+            far_copy(span, 0, step).start()
         diagonal = lax.broadcasted_iota(jnp.int32, (rows, rows), 0) == lax.broadcasted_iota(
             jnp.int32, (rows, rows), 1
         )
@@ -365,9 +367,8 @@
             jnp.where(diagonal, rate_ref[pl.ds(span, 1), :], 0.0), axis=1, keepdims=True
         )
         both[span, 1, own, :] = (-rates * (sums[1] * scale)).astype(jnp.bfloat16)
-        for part in range(2):
-            for step in range(1, chips):
-                far_copy(span, part, step).start()
+        for step in range(1, chips):
+            far_copy(span, 1, step).start()
         for part in range(2):
             near_copy(span, part, 0).start()
 

time: 133 us -> 133 us (level)
  no operation moved by 1% of the time
where the time goes in v7:
time: 133 us
  Pallas kernels  131 us (98%)
  local copies, waits for them, and re-layouts  1.87 us (1%)
    pallas_call x1, Pallas kernels, shards(): pl.pallas_call(functools.partial(step_kernel, segments, devices, heads, c...  131 us

profile of v7, /device:TPU:3, one launch (start us, length us, event | category | flops | bytes accessed | tf_op | source)
XLA Modules:
  0.0 133.2 jit_solution(3730619985218507449)
XLA Ops:
  0.0 131.4 %step.1 = bf16[2,128,1024]{2,1,0:T(8,128)(2,1)} custom-call(bf16[2,128,1024]{2,1,0:T(8,128)(2,1)} %stream_hbm.1, f32[1,4096]{1,0:T(1,128)} %in_gain_ref.1, bf16[3,4096,512]{2,1,0:T(8,128)(2,1)} %bitcast.11, f32[2,512]{1,0:T(2,128)} %bitcast.17, bf16[512,768]{1,0:T(8,128)(2,1)} %bitcast.14, bf16[512,768]{1,0:T(8,128)(2,1)} %bitcast.15, ...), custom_call_target="tpu_custom_call" | custom-call | tf_op jit(solution)/shard_map/step/pallas_call | solution.py:810
  131.4 1.9 %copy.12 = bf16[1,2,128,1024]{3,2,1,0:T(8,128)(2,1)} copy(bf16[1,2,128,1024]{3,2,1,0:T(8,128)(2,1)} %bitcast.13) | data formatting | bytes 1048576
